TPU v7x, 32 devices: a whole 2x2x4 slice. The times are simulated.
32 devices in a mesh: groups: 2 (over y), tensor: 4 (over z), store: 4 (over x, core).
Axes of the slice: x: 2, y: 2, z: 4, core: 2. Of those that a mesh axis runs over, the one named last changes fastest.
Arguments:
- tokens: bfloat16 [4096, 8192], P(('groups', 'store', 'tensor')), parts along dimension 0, may hold values from -32 to 32
- query_weight: bfloat16 [8192, 8192], P(None, 'tensor'), may hold values from -0.0625 to 0.0625
- key_value_weight: bfloat16 [8192, 2048], P(None, 'tensor'), may hold values from -0.0625 to 0.0625
- adapter_down_maps: bfloat16 [32, 128, 8192], P('store', None, 'tensor'), may hold values from -0.0625 to 0.0625
- adapter_up_query: bfloat16 [32, 64, 8192], P('store', None, 'tensor'), may hold values from -0.375 to 0.375
- adapter_up_key_value: bfloat16 [32, 64, 2048], P('store', None, 'tensor'), may hold values from -0.375 to 0.375
- adapter_row_table: int32 [64], P('groups'), parts along dimension 0, may hold values from 0 to 31, as said below
- request_adapter_ids: int32 [8, 4], P('groups'), parts along dimension 0, may hold values from 0 to 31, as said below
- token_request_ids: int32 [8, 512], P(('groups', 'store')), parts along dimension 0, may hold values from 0 to 3, never falling along the last dimension, each value on 1 to 256 neighbouring positions
Outputs:
- attention: bfloat16 [4096, 8192], P(('groups', 'store'), 'tensor'), parts along dimension 0
There are 2 independent parts, one for each index of `groups`. A program takes and returns all parts, laid end to end along the dimension named above; an argument that names none is the same for every part. Nothing has to cross between parts.
Inputs may be any that keep to these rules, and one draw needn't show every extreme that they name: A permutation: adapter a lies in row adapter_row_table[a] of the adapter arrays, on store index adapter_row_table[a] // 8. `request_adapter_ids`: the 4 requests of one store batch use adapters held on 4 different store indices. `token_request_ids`: requests are contiguous runs of a store batch, each of 1 to 256 tokens.
All inputs are finite; a program needn't handle non-finite values.
Results may differ from a plain program's by a relative error of at most 0.012.
The roundings to bfloat16 on the way count: a program that leaves them out, or rounds other values in their place, can miss the bound.
Values may be sent and summed in bfloat16 or wider, within the bound.
A program may use at most 128 MiB of HBM per device.

v0:
```python
import functools
import math

import jax
import jax.numpy as jnp
from jax import lax
from jax.experimental import pallas as pl
from jax.experimental.pallas import tpu as pltpu
from jax.sharding import PartitionSpec as P

MODEL_WIDTH = 8192
QUERY_HEADS = 64
KEY_VALUE_HEADS = 8
HEAD_SIZE = 128
ADAPTER_RANK = 64
STORE_REQUESTS = 4
TOK_ST = 512


adapter_scale = 2.0
rope_theta = 500000.0


MAX_RUN = 256
MESH = pl.DeviceIdType.MESH


def select_kernel(
    position_count, table_ref, request_ref, down_hbm, query_hbm, keyval_hbm, *rest
):
    outs, held, in_sem, out_sem = rest[:3], rest[3:6], rest[6], rest[7]
    s = lax.axis_index("store")
    stacks = (down_hbm, query_hbm, keyval_hbm)
    loads = []
    for i in range(request_ref.shape[0]):
        index = 0
        for k in range(STORE_REQUESTS):
            slot = table_ref[request_ref[i, k]]
            index += jnp.where(
                lax.div(slot, position_count) == s, lax.rem(slot, position_count), 0
            )
        for j in range(3):
            copy = pltpu.make_async_copy(stacks[j].at[index], held[j].at[i], in_sem.at[j, i])
            copy.start()
            loads.append((j, i, copy))
    stores = []
    for j, i, copy in loads:
        copy.wait()
        store = pltpu.make_async_copy(held[j].at[i], outs[j].at[i], out_sem.at[j, i])
        store.start()
        stores.append(store)
    for store in stores:
        store.wait()


def select_adapters(table, requests, stacks):
    hbm = pl.BlockSpec(memory_space=pl.ANY)
    smem = pl.BlockSpec(memory_space=pltpu.SMEM)
    count = requests.shape[0]
    shapes = [(count,) + stack.shape[1:] for stack in stacks]
    return pl.pallas_call(
        functools.partial(select_kernel, stacks[0].shape[0]),
        in_specs=[smem, smem] + [hbm] * 3,
        out_specs=[hbm] * 3,
        out_shape=[jax.ShapeDtypeStruct(shape, jnp.bfloat16) for shape in shapes],
        scratch_shapes=[pltpu.VMEM(shape, jnp.bfloat16) for shape in shapes]
        + [pltpu.SemaphoreType.DMA((3, count)), pltpu.SemaphoreType.DMA((3, count))],
        name="select_adapters",
    )(table, requests, *stacks)


def project_kernel(
    n,
    stores,
    chunks,
    position_count,
    tokens_ref,
    wq_hbm,
    wkv_hbm,
    down_hbm,
    upq_hbm,
    upkv_hbm,
    table_ref,
    request_ref,
    segment_ref,
    out_ref,
    xbuf,
    wq,
    wkv,
    acc_q,
    acc_kv,
    down,
    upq,
    upkv,
    low_part,
    low_own,
    low_got,
    low_all,
    kv_heads,
    kv_got,
    keys_ref,
    values_ref,
    bias_ref,
    cos_ref,
    sin_ref,
    holder_ref,
    token_sem,
    weight_sem,
    recv_sem,
    send_sem,
    adapter_send,
    adapter_recv,
    adapter_own,
    part_send,
    part_recv,
    low_send,
    low_recv,
    kv_sem,
    out_sem,
):
    t = lax.axis_index("tensor")
    s = lax.axis_index("store")
    rows = tokens_ref.shape[0]
    width = tokens_ref.shape[1] // chunks
    total = rows * n
    query_width = wq.shape[1]
    keyval_width = wkv.shape[1]
    pair_heads = keyval_width // HEAD_SIZE
    head_local = query_width // HEAD_SIZE
    group_size = QUERY_HEADS // KEY_VALUE_HEADS
    kv_used = max(head_local // group_size, 1)

    def kv_first(rank):
        return rank * head_local // group_size - rank // 2 * pair_heads

    barrier = pltpu.get_barrier_semaphore()
    for d in range(1, n):
        pl.semaphore_signal(
            barrier, inc=1, device_id={"tensor": lax.rem(t + d, n)}, device_id_type=MESH
        )
    for d in range(1, stores):
        pl.semaphore_signal(
            barrier, inc=1, device_id={"store": lax.rem(s + d, stores)}, device_id_type=MESH
        )

    def own_copy(c):
        return pltpu.make_async_copy(
            tokens_ref.at[:, pl.ds(c * width, width)],
            xbuf.at[c, pl.ds(t * rows, rows), :],
            token_sem.at[c],
        )

    def weight_copies(c):
        part = pl.ds(c * width, width)
        return (
            pltpu.make_async_copy(wq_hbm.at[part, :], wq.at[part, :], weight_sem.at[0, c]),
            pltpu.make_async_copy(wkv_hbm.at[part, :], wkv.at[part, :], weight_sem.at[1, c]),
        )

    for c in range(chunks):
        own_copy(c).start()
        for copy in weight_copies(c):
            copy.start()
    adapter_pairs = ((down_hbm, down), (upq_hbm, upq), (upkv_hbm, upkv))

    def adapter_block(held, i, at):
        if i == 0:
            return held.at[at]
        return held.at[pl.ds(at * ADAPTER_RANK, ADAPTER_RANK), :]

    own_adapters = [
        pltpu.make_async_copy(source.at[s], adapter_block(held, i, s), adapter_own.at[i])
        for i, (source, held) in enumerate(adapter_pairs)
    ]
    for copy in own_adapters:
        copy.start()

    pl.semaphore_wait(barrier, n - 1 + stores - 1)

    def place(side, i):
        return chunks - 1 - i if side == 0 else i

    def stream_copy(side, p, i, own):
        c = place(side, i)
        shard = t - p if side == 0 else t + p
        held = xbuf.at[c, pl.ds(shard * rows, rows), :]
        source = tokens_ref.at[:, pl.ds(c * width, width)] if own else held
        return pltpu.make_async_remote_copy(
            src_ref=source,
            dst_ref=held,
            send_sem=send_sem.at[side, p, i],
            recv_sem=recv_sem.at[side, p, i],
            device_id={"tensor": t + 1 if side == 0 else t - 1},
            device_id_type=MESH,
        )

    def arrival(side, p, i):
        c = place(side, i)
        shard = t - p if side == 0 else t + p
        held = xbuf.at[c, pl.ds(shard * rows, rows), :]
        return pltpu.make_async_remote_copy(
            src_ref=held,
            dst_ref=held,
            send_sem=send_sem.at[side, p - 1, i],
            recv_sem=recv_sem.at[side, p - 1, i],
            device_id={"tensor": t - 1 if side == 0 else t + 1},
            device_id_type=MESH,
        )

    can_send = (t < n - 1, t > 0)
    for i in range(chunks):
        for side in range(2):

            @pl.when(can_send[side])
            def _():
                stream_copy(side, 0, i, True).start()

    adapter_sends = []
    for d in range(1, stores):
        for i, (source, held) in enumerate(adapter_pairs):
            peer = lax.rem(s + d, stores)
            copy = pltpu.make_async_remote_copy(
                src_ref=source.at[peer],
                dst_ref=adapter_block(held, i, s),
                send_sem=adapter_send.at[i, d],
                recv_sem=adapter_recv.at[i, d],
                device_id={"store": peer},
                device_id_type=MESH,
            )
            copy.start()
            adapter_sends.append(copy)

    tile_q = min(query_width, 512)

    def unit(c, shard, first):
        at = pl.ds(pl.multiple_of(shard * rows, rows), rows)
        part = pl.ds(pl.multiple_of(c * width, width), width)
        x = xbuf[c, at, :]
        add = jnp.dot(x, wkv[part, :], preferred_element_type=jnp.float32)
        if first:
            acc_kv[at, :] = add
        else:
            acc_kv[at, :] += add

        @pl.loop(0, query_width // tile_q)
        def _(k):
            columns = pl.ds(pl.multiple_of(k * tile_q, tile_q), tile_q)
            more = jnp.dot(
                xbuf[c, at, :], wq[part, columns], preferred_element_type=jnp.float32
            )
            if first:
                acc_q[at, columns] = more
            else:
                acc_q[at, columns] += more

    acc_q[...] = jnp.zeros_like(acc_q)
    acc_kv[...] = jnp.zeros_like(acc_kv)
    holds_keys = t % 2 == 0

    place_row = lax.broadcasted_iota(jnp.int32, (total, total), 0)
    place_column = lax.broadcasted_iota(jnp.int32, (total, total), 1)
    across = segment_ref[...].astype(jnp.float32)
    down_column = jnp.sum(jnp.where(place_row == place_column, across, 0.0), axis=1, keepdims=True)
    allowed = jnp.logical_and(down_column == across, place_row >= place_column)
    bias_ref[...] = jnp.where(allowed, 0.0, -1e30)
    first_index = jnp.sum(jnp.where(across < down_column, 1.0, 0.0), axis=1, keepdims=True)
    place_token = lax.broadcasted_iota(jnp.int32, (total, 1), 0).astype(jnp.float32)
    lane = lax.broadcasted_iota(jnp.int32, (total, HEAD_SIZE), 1)
    exponent = lax.rem(lane, HEAD_SIZE // 2).astype(jnp.float32) * (2.0 / HEAD_SIZE)
    angles = (place_token - first_index) * jnp.exp(-exponent * math.log(rope_theta))
    sine = jnp.sin(angles)
    cos_ref[...] = jnp.cos(angles)
    sin_ref[...] = jnp.where(lane < HEAD_SIZE // 2, -sine, sine)
    holder = jnp.zeros((total, 1), jnp.float32)
    for k in range(STORE_REQUESTS):
        owner = lax.div(table_ref[request_ref[s, k]], position_count).astype(jnp.float32)
        holder += jnp.where(down_column == float(k), owner, 0.0)
    holder_ref[...] = holder

    def mask_of(p):
        return jnp.where(holder_ref[...] == float(p), 1.0, 0.0)

    @pl.loop(0, chunks)
    def _(c):
        own_copy(c).wait()
        for copy in weight_copies(c):
            copy.wait()
        unit(c, t, False)

    for copy in own_adapters:
        copy.wait()

    share = chunks // n
    last_phase = jnp.maximum(t, n - 1 - t)
    low_at = share * (jnp.minimum(t, n - 1 - t) + 1) - 1

    def part_copy(d):
        to = lax.rem(t + d, n)
        return pltpu.make_async_remote_copy(
            src_ref=low_part.at[pl.ds(to * rows, rows), :],
            dst_ref=low_got.at[t],
            send_sem=part_send.at[d],
            recv_sem=part_recv.at[d],
            device_id={"tensor": to},
            device_id_type=MESH,
        )

    def part_arrival(d):
        source = lax.rem(t + n - d, n)
        return pltpu.make_async_remote_copy(
            src_ref=low_got.at[source],
            dst_ref=low_got.at[source],
            send_sem=part_send.at[d],
            recv_sem=part_recv.at[d],
            device_id={"tensor": source},
            device_id_type=MESH,
        )

    def low_copy(d):
        to = lax.rem(t + d, n)
        held = low_all.at[pl.ds(t * rows, rows), :]
        return pltpu.make_async_remote_copy(
            src_ref=held,
            dst_ref=held,
            send_sem=low_send.at[d],
            recv_sem=low_recv.at[d],
            device_id={"tensor": to},
            device_id_type=MESH,
        )

    def low_arrival(d):
        source = lax.rem(t + n - d, n)
        held = low_all.at[pl.ds(source * rows, rows), :]
        return pltpu.make_async_remote_copy(
            src_ref=held,
            dst_ref=held,
            send_sem=low_send.at[d],
            recv_sem=low_recv.at[d],
            device_id={"tensor": source},
            device_id_type=MESH,
        )

    def adapters_arrive():
        for d in range(1, stores):
            source = lax.rem(s + stores - d, stores)
            for i, (_, held) in enumerate(adapter_pairs):
                block = adapter_block(held, i, source)
                pltpu.make_async_remote_copy(
                    src_ref=block,
                    dst_ref=block,
                    send_sem=adapter_send.at[i, d],
                    recv_sem=adapter_recv.at[i, d],
                    device_id={"store": source},
                    device_id_type=MESH,
                ).wait_recv()

    def low_first():
        adapters_arrive()
        summed = jnp.zeros(low_part.shape, jnp.float32)
        for p in range(stores):
            picked = jnp.zeros(low_part.shape, jnp.float32)
            for k in range(share):
                picked += lax.dot_general(
                    xbuf[t * share + k],
                    down[p, :, k * width : (k + 1) * width],
                    (((1,), (1,)), ((), ())),
                    preferred_element_type=jnp.float32,
                )
            summed += picked * mask_of(p)
        low_part[...] = summed.astype(jnp.bfloat16)
        low_own[...] = summed
        for d in range(1, n):
            part_copy(d).start()

    def low_second():
        at = pl.ds(pl.multiple_of(t * rows, rows), rows)
        whole = low_own[at, :]
        for d in range(1, n):
            part_arrival(d).wait_recv()
            whole += low_got[lax.rem(t + n - d, n)].astype(jnp.float32)
        low_all[at, :] = whole.astype(jnp.bfloat16)
        for d in range(1, n):
            low_copy(d).start()

    def low_third():
        for d in range(1, n):
            low_arrival(d).wait_recv()
        low = low_all[...].astype(jnp.float32)
        turned = pltpu.roll(low, ADAPTER_RANK, 1)
        in_lower = lax.broadcasted_iota(jnp.int32, low.shape, 1) < ADAPTER_RANK
        twice_q = jnp.where(in_lower, low, turned)
        twice_kv = jnp.where(in_lower, turned, low)
        masks = [
            jnp.where(in_lower, mask_of(2 * p), mask_of(2 * p + 1))
            for p in range(stores // 2)
        ]
        spread_q = jnp.concatenate([(twice_q * m).astype(jnp.bfloat16) for m in masks], axis=1)
        spread_kv = jnp.concatenate([(twice_kv * m).astype(jnp.bfloat16) for m in masks], axis=1)
        acc_kv[...] += adapter_scale * jnp.dot(
            spread_kv, upkv[...], preferred_element_type=jnp.float32
        )
        for k in range(query_width // tile_q):
            columns = slice(k * tile_q, (k + 1) * tile_q)
            acc_q[:, columns] += adapter_scale * jnp.dot(
                spread_q, upq[:, columns], preferred_element_type=jnp.float32
            )

    def rotated(value, cosine, sine):
        return value * cosine + pltpu.roll(value, HEAD_SIZE // 2, 1) * sine

    ends_first = t >= n - t
    early_start = pl.multiple_of(jnp.where(ends_first, rows, 0), rows)
    late_start = pl.multiple_of(jnp.where(ends_first, 0, total - rows), rows)
    partner = t + 1 - 2 * (t % 2)

    def finish_keyval(start, count):
        at = pl.ds(start, count)
        cosine = jnp.where(holds_keys, cos_ref[at, :], 1.0)
        sine = jnp.where(holds_keys, sin_ref[at, :], 0.0)
        for m in range(pair_heads):
            value = acc_kv[at, m * HEAD_SIZE : (m + 1) * HEAD_SIZE]
            kv_heads[m, at, :] = rotated(value, cosine, sine).astype(jnp.bfloat16)

    def keyval_copy(start, count, which):
        at = pl.ds(start, count)
        return pltpu.make_async_remote_copy(
            src_ref=kv_heads.at[pl.ds(kv_first(partner), kv_used), at, :],
            dst_ref=kv_got.at[:, at, :],
            send_sem=kv_sem.at[0, which],
            recv_sem=kv_sem.at[1, which],
            device_id={"tensor": partner},
            device_id_type=MESH,
        )

    depth = min(4, chunks)

    @pl.loop(0, (n - 1) * chunks)
    def _(step):
        p = step // chunks + 1
        i = step % chunks
        here = (t - p >= 0, t + p < n)
        for side in range(2):

            @pl.when(jnp.logical_and(here[side], can_send[side]))
            def _():
                back = step + chunks - depth
                arrival(side, p, i).wait_recv()
                stream_copy(side, back // chunks, back % chunks, False).wait_send()
                stream_copy(side, p, i, False).start()

            @pl.when(jnp.logical_and(here[side], jnp.logical_not(can_send[side])))
            def _():
                arrival(side, p, i).wait_recv()

        for side in range(2):

            @pl.when(here[side])
            def _():
                unit(place(side, i), t - p if side == 0 else t + p, False)

        @pl.when(jnp.logical_and(p == last_phase, i == low_at))
        def _():
            low_first()

        @pl.when(jnp.logical_and(p == last_phase, i == low_at + 1))
        def _():
            low_second()

        @pl.when(jnp.logical_and(p == last_phase, i == chunks - 2))
        def _():
            low_third()
            finish_keyval(early_start, total - rows)
            keyval_copy(early_start, total - rows, 0).start()

    finish_keyval(late_start, rows)
    keyval_copy(late_start, rows, 1).start()
    for copy in adapter_sends:
        copy.wait_send()
    for d in range(1, n):
        part_copy(d).wait_send()
        low_copy(d).wait_send()

    @pl.loop(0, chunks - depth)
    def _(k):
        for side in range(2):

            @pl.when(can_send[side])
            def _():
                stream_copy(side, 0, k, False).wait_send()

    @pl.loop(0, depth)
    def _(k):
        for side in range(2):

            @pl.when(can_send[side])
            def _():
                reach = t if side == 0 else n - 1 - t
                back = (reach + 1) * chunks - depth + k
                stream_copy(side, back // chunks, back % chunks, False).wait_send()

    per_chunk = width // HEAD_SIZE
    for h in range(head_local):
        columns = slice(h * HEAD_SIZE, (h + 1) * HEAD_SIZE)
        inside = h % per_chunk * HEAD_SIZE
        xbuf[h // per_chunk, :, inside : inside + HEAD_SIZE] = rotated(
            acc_q[:, columns], cos_ref[...], sin_ref[...]
        ).astype(jnp.bfloat16)

    keyval_copy(early_start, total - rows, 0).wait()
    keyval_copy(late_start, rows, 1).wait()
    own_first = kv_first(t)
    for g in range(kv_used):
        values_ref[g, :, HEAD_SIZE:] = jnp.ones((total, HEAD_SIZE), jnp.bfloat16)

        @pl.when(holds_keys)
        def _():
            keys_ref[g] = kv_heads[own_first + g]
            values_ref[g, :, :HEAD_SIZE] = kv_got[g]

        @pl.when(jnp.logical_not(holds_keys))
        def _():
            keys_ref[g] = kv_got[g]
            values_ref[g, :, :HEAD_SIZE] = kv_heads[own_first + g]

    per_kv = head_local // kv_used
    batch = min(8, per_kv, per_chunk)
    batches_per_chunk = per_chunk // batch
    block = 128
    scale = 1.0 / math.sqrt(HEAD_SIZE) / math.log(2.0)

    def out_copy(q):
        whole = pl.multiple_of(q * batch * HEAD_SIZE, batch * HEAD_SIZE)
        return pltpu.make_async_copy(
            wq.at[pl.ds(0, total), pl.ds(whole, batch * HEAD_SIZE)],
            out_ref.at[:, pl.ds(whole, batch * HEAD_SIZE)],
            out_sem.at[q],
        )

    @pl.loop(0, head_local // batch)
    def _(q):
        chunk = q // batches_per_chunk
        base = q % batches_per_chunk * batch
        g = q * batch // per_kv
        for pair in range(batch // 2):
            lanes = [
                pl.ds(pl.multiple_of((base + 2 * pair + k) * HEAD_SIZE, HEAD_SIZE), HEAD_SIZE)
                for k in range(2)
            ]
            out_lanes = [
                pl.ds(
                    pl.multiple_of((q * batch + 2 * pair + k) * HEAD_SIZE, HEAD_SIZE), HEAD_SIZE
                )
                for k in range(2)
            ]
            for b in range(total // block):
                low = max(0, b * block - MAX_RUN)
                high = (b + 1) * block
                at = slice(b * block, high)
                stacked = jnp.concatenate([xbuf[chunk, at, ln] for ln in lanes], axis=0)
                scores = lax.dot_general(
                    stacked,
                    keys_ref[g, low:high, :],
                    (((1,), (1,)), ((), ())),
                    preferred_element_type=jnp.float32,
                )
                scores = scores.reshape(2, block, high - low) + bias_ref[at, low:high][None]
                scores = (scores - jnp.max(scores, axis=2, keepdims=True)) * scale
                weights = jnp.exp2(scores).astype(jnp.bfloat16).reshape(2 * block, high - low)
                mixed = jnp.dot(
                    weights, values_ref[g, low:high, :], preferred_element_type=jnp.float32
                )
                mixed = (mixed[:, :HEAD_SIZE] / mixed[:, HEAD_SIZE:]).astype(jnp.bfloat16)
                for k in range(2):
                    wq[at, out_lanes[k]] = mixed[k * block : (k + 1) * block]
        out_copy(q).start()

    @pl.loop(0, head_local // batch)
    def _(q):
        out_copy(q).wait()


def on_device(
    tokens,
    query_weight,
    key_value_weight,
    adapter_down_maps,
    adapter_up_query,
    adapter_up_key_value,
    adapter_row_table,
    request_adapter_ids,
    token_request_ids,
):
    n = lax.axis_size("tensor")
    stores = lax.axis_size("store")
    position_count = adapter_down_maps.shape[0]
    down, up_query, up_keyval = select_adapters(
        adapter_row_table,
        request_adapter_ids,
        (adapter_down_maps, adapter_up_query, adapter_up_key_value),
    )
    rows, model_width = tokens.shape
    total = rows * n
    query_width = query_weight.shape[1]
    keyval_width = key_value_weight.shape[1]
    chunks = max(8, n)
    width = model_width // chunks
    pair_heads = keyval_width // HEAD_SIZE
    kv_used = max(query_width // HEAD_SIZE // (QUERY_HEADS // KEY_VALUE_HEADS), 1)
    two_ranks = 2 * ADAPTER_RANK
    hbm = pl.BlockSpec(memory_space=pl.ANY)
    vmem = pl.BlockSpec(memory_space=pltpu.VMEM)
    smem = pl.BlockSpec(memory_space=pltpu.SMEM)
    dma = pltpu.SemaphoreType.DMA
    return pl.pallas_call(
        functools.partial(project_kernel, n, stores, chunks, position_count),
        in_specs=[hbm] * 6 + [smem, smem, vmem],
        out_specs=hbm,
        out_shape=jax.ShapeDtypeStruct((total, query_width), jnp.bfloat16),
        scratch_shapes=[
            pltpu.VMEM((chunks, total, width), jnp.bfloat16),
            pltpu.VMEM((model_width, query_width), jnp.bfloat16),
            pltpu.VMEM((model_width, keyval_width), jnp.bfloat16),
            pltpu.VMEM((total, query_width), jnp.float32),
            pltpu.VMEM((total, keyval_width), jnp.float32),
            pltpu.VMEM((stores, two_ranks, model_width // n), jnp.bfloat16),
            pltpu.VMEM((stores * ADAPTER_RANK, query_width), jnp.bfloat16),
            pltpu.VMEM((stores * ADAPTER_RANK, keyval_width), jnp.bfloat16),
            pltpu.VMEM((total, two_ranks), jnp.bfloat16),
            pltpu.VMEM((total, two_ranks), jnp.float32),
            pltpu.VMEM((n, rows, two_ranks), jnp.bfloat16),
            pltpu.VMEM((total, two_ranks), jnp.bfloat16),
            pltpu.VMEM((pair_heads, total, HEAD_SIZE), jnp.bfloat16),
            pltpu.VMEM((kv_used, total, HEAD_SIZE), jnp.bfloat16),
            pltpu.VMEM((kv_used, total, HEAD_SIZE), jnp.bfloat16),
            pltpu.VMEM((kv_used, total, 2 * HEAD_SIZE), jnp.bfloat16),
            pltpu.VMEM((total, total), jnp.float32),
            pltpu.VMEM((total, HEAD_SIZE), jnp.float32),
            pltpu.VMEM((total, HEAD_SIZE), jnp.float32),
            pltpu.VMEM((total, 1), jnp.float32),
            dma((chunks,)),
            dma((2, chunks)),
            dma((2, n, chunks)),
            dma((2, n, chunks)),
            dma((3, stores)),
            dma((3, stores)),
            dma((3,)),
            dma((n,)),
            dma((n,)),
            dma((n,)),
            dma((n,)),
            dma((2, 2)),
            dma((query_width // HEAD_SIZE // 4,)),
        ],
        compiler_params=pltpu.CompilerParams(
            collective_id=0, has_side_effects=True, vmem_limit_bytes=67043328
        ),
        name="project",
    )(
        tokens,
        query_weight,
        key_value_weight,
        down,
        up_query,
        up_keyval,
        adapter_row_table,
        request_adapter_ids,
        token_request_ids,
    )


def solution(mesh):
    return jax.shard_map(
        on_device,
        mesh=mesh,
        in_specs=(
            P(("groups", "store", "tensor"), None),
            P(None, "tensor"),
            P(None, "tensor"),
            P("store", None, "tensor"),
            P("store", None, "tensor"),
            P("store", None, "tensor"),
            P("groups"),
            P("groups", None),
            P(("groups", "store"), None),
        ),
        out_specs=P(("groups", "store"), "tensor"),
        check_vma=False,
    )
```

profile of v0, /device:TPU:0, one launch (start us, length us, event | category | flops | bytes accessed | tf_op | source)
XLA Modules:
  0.0 171.8 jit_solution(883545038286717330)
XLA Ops:
  0.0 4.5 %select_adapters.1 = (bf16[4,128,2048]{2,1,0:T(8,128)(2,1)}, bf16[4,64,2048]{2,1,0:T(8,128)(2,1)}, bf16[4,64,512]{2,1,0:T(8,128)(2,1)}) custom-call(s32[32]{0:T(128)} %table_ref.3, s32[4,4]{1,0:T(4,128)} %request_ref.3, bf16[8,128,2048]{2,1,0:T(8,128)(2,1)} %down_hbm.1, bf16[8,64,2048]{2,1,0:T(8,128)(2,1)} %query_hbm.1, bf16[8,64,512]{2,1,0:T(8,128)(2,1)} %keyval_hbm.1), custom_call_target="tpu_custom_call" | custom-call | tf_op jit(solution)/shard_map/select_adapters/pallas_call | solution.py:61
  4.5 164.2 %project.1 = bf16[512,2048]{1,0:T(8,128)(2,1)} custom-call(bf16[128,8192]{1,0:T(8,128)(2,1)} %tokens_ref.1, bf16[8192,2048]{1,0:T(8,128)(2,1)} %wq_hbm.1, bf16[8192,512]{1,0:T(8,128)(2,1)} %wkv_hbm.1, bf16[4,128,2048]{2,1,0:T(8,128)(2,1)} %get-tuple-element.8.down_hbm, bf16[4,64,2048]{2,1,0:T(8,128)(2,1)} %get-tuple-element.9.upq_hbm, ...), custom_call_target="tpu_custom_call" | custom-call | tf_op jit(solution)/shard_map/project/pallas_call | solution.py:614
  168.7 3.2 %copy.11 = bf16[512,2048]{1,0:T(8,128)(2,1)} copy(bf16[512,2048]{1,0:T(8,128)(2,1)} %project.1) | data formatting | bytes 4194304
where the time goes:
time: 172 us
  Pallas kernels  169 us (98%)
  local copies, waits for them, and re-layouts  3.16 us (2%)
    pallas_call x1, Pallas kernels, on_device(): pl.pallas_call(functools.partial(project_kernel, n, stores, chunks, posit...  164 us
    pallas_call x1, Pallas kernels, select_adapters(): pl.pallas_call(functools.partial(select_kernel, stacks[0].shape[0]), in_s...  4.48 us

commit v1 on v0

v1 whole, which is shorter than its diff:
```python
import functools
import math

import jax
import jax.numpy as jnp
from jax import lax
from jax.experimental import pallas as pl
from jax.experimental.pallas import tpu as pltpu
from jax.sharding import PartitionSpec as P

MODEL_WIDTH = 8192
QUERY_HEADS = 64
KEY_VALUE_HEADS = 8
HEAD_SIZE = 128
ADAPTER_RANK = 64
STORE_REQUESTS = 4
TOK_ST = 512


adapter_scale = 2.0
rope_theta = 500000.0


MAX_RUN = 256
MESH = pl.DeviceIdType.MESH


def project_kernel(
    n,
    stores,
    chunks,
    slots,
    tokens_ref,
    wq_hbm,
    wkv_hbm,
    down_hbm,
    upq_hbm,
    upkv_hbm,
    table_ref,
    request_ref,
    segment_ref,
    out_ref,
    down_picked,
    upq_picked,
    upkv_picked,
    xbuf,
    wq,
    wkv,
    acc_q,
    acc_kv,
    down,
    upq,
    upkv,
    low_part,
    low_own,
    low_got,
    low_all,
    kv_heads,
    kv_got,
    keys_ref,
    values_ref,
    bias_ref,
    cos_ref,
    sin_ref,
    holder_ref,
    token_sem,
    weight_sem,
    recv_sem,
    send_sem,
    adapter_send,
    adapter_recv,
    adapter_own,
    candidate_sem,
    picked_sem,
    part_send,
    part_recv,
    low_send,
    low_recv,
    kv_sem,
    out_sem,
):
    t = lax.axis_index("tensor")
    s = lax.axis_index("store")
    rows = tokens_ref.shape[0]
    width = tokens_ref.shape[1] // chunks
    total = rows * n
    query_width = wq.shape[1]
    keyval_width = wkv.shape[1]
    pair_heads = keyval_width // HEAD_SIZE
    head_local = query_width // HEAD_SIZE
    group_size = QUERY_HEADS // KEY_VALUE_HEADS
    kv_used = max(head_local // group_size, 1)

    def kv_first(rank):
        return rank * head_local // group_size - rank // 2 * pair_heads

    barrier = pltpu.get_barrier_semaphore()
    for d in range(1, n):
        pl.semaphore_signal(
            barrier, inc=1, device_id={"tensor": lax.rem(t + d, n)}, device_id_type=MESH
        )
    for d in range(1, stores):
        pl.semaphore_signal(
            barrier, inc=1, device_id={"store": lax.rem(s + d, stores)}, device_id_type=MESH
        )

    def own_copy(c):
        return pltpu.make_async_copy(
            tokens_ref.at[:, pl.ds(c * width, width)],
            xbuf.at[c, pl.ds(t * rows, rows), :],
            token_sem.at[c],
        )

    def weight_copies(c):
        part = pl.ds(c * width, width)
        return (
            pltpu.make_async_copy(wq_hbm.at[part, :], wq.at[part, :], weight_sem.at[0, c]),
            pltpu.make_async_copy(wkv_hbm.at[part, :], wkv.at[part, :], weight_sem.at[1, c]),
        )

    model_width = wq.shape[0]
    two_ranks = 2 * ADAPTER_RANK
    picked_down = chunks // 2 * width
    picked_up = picked_down + stores * two_ranks
    picked_end = picked_up + stores * ADAPTER_RANK
    candidate_sets = (
        (down_hbm, wq, 0, two_ranks, picked_down, down_picked),
        (upq_hbm, wq, slots * two_ranks, ADAPTER_RANK, picked_up, upq_picked),
        (upkv_hbm, wkv, 0, ADAPTER_RANK, picked_up, upkv_picked),
    )
    candidates = [
        pltpu.make_async_copy(
            source.at[k], held.at[pl.ds(first + k * count, count), :], candidate_sem.at[j, k]
        )
        for j, (source, held, first, count, _, _) in enumerate(candidate_sets)
        for k in range(slots)
    ]
    adapter_pairs = ((down_picked, down), (upq_picked, upq), (upkv_picked, upkv))

    def adapter_block(held, i, at):
        if i == 0:
            return held.at[at]
        return held.at[pl.ds(at * ADAPTER_RANK, ADAPTER_RANK), :]

    own_adapters = [
        pltpu.make_async_copy(source.at[s], adapter_block(held, i, s), adapter_own.at[i])
        for i, (source, held) in enumerate(adapter_pairs)
    ]

    pl.semaphore_wait(barrier, n - 1 + stores - 1)

    def place(side, i):
        return chunks - 1 - i if side == 0 else i

    def stream_copy(side, p, i, own):
        c = place(side, i)
        shard = t - p if side == 0 else t + p
        held = xbuf.at[c, pl.ds(shard * rows, rows), :]
        source = tokens_ref.at[:, pl.ds(c * width, width)] if own else held
        return pltpu.make_async_remote_copy(
            src_ref=source,
            dst_ref=held,
            send_sem=send_sem.at[side, p, i],
            recv_sem=recv_sem.at[side, p, i],
            device_id={"tensor": t + 1 if side == 0 else t - 1},
            device_id_type=MESH,
        )

    def arrival(side, p, i):
        c = place(side, i)
        shard = t - p if side == 0 else t + p
        held = xbuf.at[c, pl.ds(shard * rows, rows), :]
        return pltpu.make_async_remote_copy(
            src_ref=held,
            dst_ref=held,
            send_sem=send_sem.at[side, p - 1, i],
            recv_sem=recv_sem.at[side, p - 1, i],
            device_id={"tensor": t - 1 if side == 0 else t + 1},
            device_id_type=MESH,
        )

    is_end = jnp.logical_or(t == 0, t == n - 1)
    share = chunks // n
    can_send = (t < n - 1, t > 0)
    reach = (t, n - 1 - t)

    def item(shards, j):
        head = share * shards
        rest = chunks - share
        in_head = j < head
        k = jnp.maximum(j - head, 0)
        return (
            jnp.where(in_head, j // share, k // rest) + 1,
            jnp.where(in_head, j % share, share + k % rest),
        )

    def send_item(side, j, own):
        p, i = item(reach[side] + 1, j)
        return stream_copy(side, p - 1, i, own)

    def start_send(side, j):
        p, i = item(reach[side] + 1, j)

        @pl.when(p == 1)
        def _():
            stream_copy(side, 0, i, True).start()

        @pl.when(p > 1)
        def _():
            stream_copy(side, p - 1, i, False).start()

    ahead = 2
    depth = 4
    for j in range(ahead):
        for side in range(2):

            @pl.when(can_send[side])
            def _():
                stream_copy(side, 0, j, True).start()

    for copy in candidates:
        copy.start()
    for c in range(chunks):
        own_copy(c).start()

    tile_q = min(query_width, 512)

    def keyval_unit(c, shard):
        at = pl.ds(pl.multiple_of(shard * rows, rows), rows)
        part = pl.ds(pl.multiple_of(c * width, width), width)
        acc_kv[at, :] += jnp.dot(
            xbuf[c, at, :], wkv[part, :], preferred_element_type=jnp.float32
        )

    def query_unit(c, shard):
        at = pl.ds(pl.multiple_of(shard * rows, rows), rows)
        part = pl.ds(pl.multiple_of(c * width, width), width)

        @pl.loop(0, query_width // tile_q)
        def _(k):
            columns = pl.ds(pl.multiple_of(k * tile_q, tile_q), tile_q)
            acc_q[at, columns] += jnp.dot(
                xbuf[c, at, :], wq[part, columns], preferred_element_type=jnp.float32
            )

    acc_q[...] = jnp.zeros_like(acc_q)
    acc_kv[...] = jnp.zeros_like(acc_kv)
    holds_keys = t % 2 == 0

    def request_column():
        place_row = lax.broadcasted_iota(jnp.int32, (total, total), 0)
        place_column = lax.broadcasted_iota(jnp.int32, (total, total), 1)
        across = segment_ref[...].astype(jnp.float32)
        own = jnp.where(place_row == place_column, across, 0.0)
        return across, jnp.sum(own, axis=1, keepdims=True), place_row >= place_column

    def fill_tables():
        across, down_column, ordered = request_column()
        allowed = jnp.logical_and(down_column == across, ordered)
        bias_ref[...] = jnp.where(allowed, 0.0, -1e30)
        first_index = jnp.sum(jnp.where(across < down_column, 1.0, 0.0), axis=1, keepdims=True)
        place_token = lax.broadcasted_iota(jnp.int32, (total, 1), 0).astype(jnp.float32)
        lane = lax.broadcasted_iota(jnp.int32, (total, HEAD_SIZE), 1)
        exponent = lax.rem(lane, HEAD_SIZE // 2).astype(jnp.float32) * (2.0 / HEAD_SIZE)
        angles = (place_token - first_index) * jnp.exp(-exponent * math.log(rope_theta))
        sine = jnp.sin(angles)
        cos_ref[...] = jnp.cos(angles)
        sin_ref[...] = jnp.where(lane < HEAD_SIZE // 2, -sine, sine)

    def fill_holder():
        _, down_column, _ = request_column()
        holder = jnp.zeros((total, 1), jnp.float32)
        for k in range(STORE_REQUESTS):
            owner = lax.div(table_ref[request_ref[s, k]], slots).astype(jnp.float32)
            holder += jnp.where(down_column == float(k), owner, 0.0)
        holder_ref[...] = holder

    for copy in candidates:
        copy.wait()
    bits = []
    for i in range(stores):
        index = 0
        for k in range(STORE_REQUESTS):
            slot = table_ref[request_ref[i, k]]
            index += jnp.where(lax.div(slot, slots) == s, lax.rem(slot, slots), 0)
        bits.append([lax.rem(lax.div(index, 1 << k), 2) == 1 for k in range(slots.bit_length())])

    def pick(held, first, count, to):
        lanes = min(held.shape[1], 512)

        @pl.loop(0, count // 16)
        def _(r):
            for at in range(0, held.shape[1], lanes):
                columns = slice(at, at + lanes)

                def tile(base, k):
                    return pl.ds(pl.multiple_of(base + k * count + r * 16, 16), 16)

                found = [held[tile(first, k), columns] for k in range(slots)]
                for i in range(stores):
                    left, level = found, 0
                    while len(left) > 1:
                        bit = bits[i][level]
                        left = [
                            jnp.where(bit, left[k + 1], left[k]) if k + 1 < len(left) else left[k]
                            for k in range(0, len(left), 2)
                        ]
                        level += 1
                    held[tile(to, i), columns] = left[0]

    for _, held, first, count, to, _ in candidate_sets:
        pick(held, first, count, to)
    picked_copies = [
        pltpu.make_async_copy(
            held.at[pl.ds(to + i * count, count), :], picked.at[i], picked_sem.at[j, i]
        )
        for j, (_, held, _, count, to, picked) in enumerate(candidate_sets)
        for i in range(stores)
    ]
    for copy in picked_copies:
        copy.start()
    def start_weights(k):
        for c in (k, chunks - 1 - k):
            for copy in weight_copies(c):
                copy.start()

    start_weights(0)
    for copy in picked_copies:
        copy.wait()
    for copy in own_adapters:
        copy.start()
    adapter_sends = []
    for d in range(1, stores):
        for i, (source, held) in enumerate(adapter_pairs):
            peer = lax.rem(s + d, stores)
            copy = pltpu.make_async_remote_copy(
                src_ref=source.at[peer],
                dst_ref=adapter_block(held, i, s),
                send_sem=adapter_send.at[i, d],
                recv_sem=adapter_recv.at[i, d],
                device_id={"store": peer},
                device_id_type=MESH,
            )
            copy.start()
            adapter_sends.append(copy)


    def mask_of(p):
        return jnp.where(holder_ref[...] == float(p), 1.0, 0.0)

    for copy in own_adapters:
        copy.wait()
    for c in range(chunks):
        own_copy(c).wait()

    def low_ready(side):
        first = share * (t if side == 1 else n - 1 - t)
        i = first + share - 1
        shards = reach[side]
        in_rest = share * shards + (shards - 1) * (chunks - share) + i - share
        return jnp.where(shards == 0, 0, jnp.where(i < share, share * shards - 1, in_rest))

    last_step = (n - 1) * chunks - 1
    inner_done = (n - 2) * chunks - 1
    second_at = inner_done + jnp.where(is_end, 1, 0)
    third_at = jnp.where(is_end, last_step - 3, inner_done + 1)
    early_at = jnp.where(is_end, last_step - 2, last_step - 3)
    low_at = jnp.maximum(jnp.maximum(low_ready(0), low_ready(1)), chunks)

    def part_copy(d):
        to = lax.rem(t + d, n)
        return pltpu.make_async_remote_copy(
            src_ref=low_part.at[pl.ds(to * rows, rows), :],
            dst_ref=low_got.at[t],
            send_sem=part_send.at[d],
            recv_sem=part_recv.at[d],
            device_id={"tensor": to},
            device_id_type=MESH,
        )

    def part_arrival(d):
        source = lax.rem(t + n - d, n)
        return pltpu.make_async_remote_copy(
            src_ref=low_got.at[source],
            dst_ref=low_got.at[source],
            send_sem=part_send.at[d],
            recv_sem=part_recv.at[d],
            device_id={"tensor": source},
            device_id_type=MESH,
        )

    def low_copy(d):
        to = lax.rem(t + d, n)
        held = low_all.at[pl.ds(t * rows, rows), :]
        return pltpu.make_async_remote_copy(
            src_ref=held,
            dst_ref=held,
            send_sem=low_send.at[d],
            recv_sem=low_recv.at[d],
            device_id={"tensor": to},
            device_id_type=MESH,
        )

    def low_arrival(d):
        source = lax.rem(t + n - d, n)
        held = low_all.at[pl.ds(source * rows, rows), :]
        return pltpu.make_async_remote_copy(
            src_ref=held,
            dst_ref=held,
            send_sem=low_send.at[d],
            recv_sem=low_recv.at[d],
            device_id={"tensor": source},
            device_id_type=MESH,
        )

    def adapters_arrive():
        for d in range(1, stores):
            source = lax.rem(s + stores - d, stores)
            for i, (_, held) in enumerate(adapter_pairs):
                block = adapter_block(held, i, source)
                pltpu.make_async_remote_copy(
                    src_ref=block,
                    dst_ref=block,
                    send_sem=adapter_send.at[i, d],
                    recv_sem=adapter_recv.at[i, d],
                    device_id={"store": source},
                    device_id_type=MESH,
                ).wait_recv()

    def low_first():
        fill_holder()
        adapters_arrive()
        summed = jnp.zeros(low_part.shape, jnp.float32)
        for p in range(stores):
            picked = jnp.zeros(low_part.shape, jnp.float32)
            for k in range(share):
                picked += lax.dot_general(
                    xbuf[t * share + k],
                    down[p, :, k * width : (k + 1) * width],
                    (((1,), (1,)), ((), ())),
                    preferred_element_type=jnp.float32,
                )
            summed += picked * mask_of(p)
        low_part[...] = summed.astype(jnp.bfloat16)
        low_own[...] = summed
        for d in range(1, n):
            part_copy(d).start()

    def low_second():
        at = pl.ds(pl.multiple_of(t * rows, rows), rows)
        whole = low_own[at, :]
        for d in range(1, n):
            part_arrival(d).wait_recv()
            whole += low_got[lax.rem(t + n - d, n)].astype(jnp.float32)
        low_all[at, :] = whole.astype(jnp.bfloat16)
        for d in range(1, n):
            low_copy(d).start()

    def low_third():
        for d in range(1, n):
            low_arrival(d).wait_recv()
        low = low_all[...].astype(jnp.float32)
        turned = pltpu.roll(low, ADAPTER_RANK, 1)
        in_lower = lax.broadcasted_iota(jnp.int32, low.shape, 1) < ADAPTER_RANK
        twice_q = jnp.where(in_lower, low, turned)
        twice_kv = jnp.where(in_lower, turned, low)
        masks = [
            jnp.where(in_lower, mask_of(2 * p), mask_of(2 * p + 1))
            for p in range(stores // 2)
        ]
        spread_q = jnp.concatenate([(twice_q * m).astype(jnp.bfloat16) for m in masks], axis=1)
        spread_kv = jnp.concatenate([(twice_kv * m).astype(jnp.bfloat16) for m in masks], axis=1)
        acc_kv[...] += adapter_scale * jnp.dot(
            spread_kv, upkv[...], preferred_element_type=jnp.float32
        )
        for k in range(query_width // tile_q):
            columns = slice(k * tile_q, (k + 1) * tile_q)
            acc_q[:, columns] += adapter_scale * jnp.dot(
                spread_q, upq[:, columns], preferred_element_type=jnp.float32
            )

    def rotated(value, cosine, sine):
        return value * cosine + pltpu.roll(value, HEAD_SIZE // 2, 1) * sine

    ends_first = t >= n - t
    early_start = pl.multiple_of(jnp.where(ends_first, rows, 0), rows)
    late_start = pl.multiple_of(jnp.where(ends_first, 0, total - rows), rows)
    partner = t + 1 - 2 * (t % 2)

    def finish_keyval(start, count):
        at = pl.ds(start, count)
        cosine = jnp.where(holds_keys, cos_ref[at, :], 1.0)
        sine = jnp.where(holds_keys, sin_ref[at, :], 0.0)
        for m in range(pair_heads):
            value = acc_kv[at, m * HEAD_SIZE : (m + 1) * HEAD_SIZE]
            kv_heads[m, at, :] = rotated(value, cosine, sine).astype(jnp.bfloat16)

    def keyval_copy(start, count, which):
        at = pl.ds(start, count)
        return pltpu.make_async_remote_copy(
            src_ref=kv_heads.at[pl.ds(kv_first(partner), kv_used), at, :],
            dst_ref=kv_got.at[:, at, :],
            send_sem=kv_sem.at[0, which],
            recv_sem=kv_sem.at[1, which],
            device_id={"tensor": partner},
            device_id_type=MESH,
        )

    own_first = kv_first(t)
    is_inner = jnp.logical_not(is_end)
    starts_first = jnp.logical_not(ends_first)
    holds_values = jnp.logical_not(holds_keys)
    early_count = total - rows
    per_kv = head_local // kv_used
    batch = min(8, per_kv)
    block = 128
    blocks = total // block
    scale = 1.0 / math.sqrt(HEAD_SIZE) / math.log(2.0)
    stage_at = pl.multiple_of(jnp.where(ends_first, model_width - total, 0), total)
    part_at = pl.multiple_of(jnp.where(ends_first, model_width - 2 * total, total), total)

    def finish_late():
        finish_keyval(late_start, rows)
        keyval_copy(late_start, rows, 1).start()

    def gather_keys(start, count):
        at = pl.ds(start, count)
        for g in range(kv_used):

            @pl.when(holds_keys)
            def _():
                keys_ref[g, at, :] = kv_heads[own_first + g, at, :]

            @pl.when(holds_values)
            def _():
                keys_ref[g, at, :] = kv_got[g, at, :]

    def gather_values(start, count):
        at = pl.ds(start, count)
        for g in range(kv_used):

            @pl.when(holds_keys)
            def _():
                values_ref[g, at, :HEAD_SIZE] = kv_got[g, at, :]

            @pl.when(holds_values)
            def _():
                values_ref[g, at, :HEAD_SIZE] = kv_heads[own_first + g, at, :]

    def lanes_of(h):
        return pl.ds(pl.multiple_of(h * HEAD_SIZE, HEAD_SIZE), HEAD_SIZE)

    def stage_rows(start, first, count):
        return pl.ds(pl.multiple_of(start + first, block), count)

    def weights_of(b, g, lanes):
        low = max(0, b * block - MAX_RUN)
        high = (b + 1) * block
        at = slice(b * block, high)
        query = [
            rotated(acc_q[at, ln], cos_ref[at, :], sin_ref[at, :]).astype(jnp.bfloat16)
            for ln in lanes
        ]
        scores = lax.dot_general(
            jnp.concatenate(query, axis=0),
            keys_ref[g, low:high, :],
            (((1,), (1,)), ((), ())),
            preferred_element_type=jnp.float32,
        )
        scores = scores.reshape(2, block, high - low) + bias_ref[at, low:high][None]
        scores = (scores - jnp.max(scores, axis=2, keepdims=True)) * scale
        return jnp.exp2(scores).astype(jnp.bfloat16).reshape(2 * block, high - low)

    def attend(b, g, lanes):
        low = max(0, b * block - MAX_RUN)
        high = (b + 1) * block
        mixed = jnp.dot(
            weights_of(b, g, lanes), values_ref[g, low:high, :], preferred_element_type=jnp.float32
        )
        mixed = (mixed[:, :HEAD_SIZE] / mixed[:, HEAD_SIZE:]).astype(jnp.bfloat16)
        for k, ln in enumerate(lanes):
            wq[stage_rows(stage_at, b * block, block), ln] = mixed[k * block : (k + 1) * block]

    def attend_part(b, g, lanes):
        high = (b + 1) * block
        weights = weights_of(b, g, lanes)
        first = weights[:, :block]
        mixed = jnp.dot(
            weights[:, block:], values_ref[g, block:high, :], preferred_element_type=jnp.float32
        )
        sums = mixed[:, HEAD_SIZE:] + jnp.dot(
            first, values_ref[g, :block, HEAD_SIZE:], preferred_element_type=jnp.float32
        )
        inverse = 1.0 / sums
        rest = mixed[:, :HEAD_SIZE] * inverse
        first = (first.astype(jnp.float32) * inverse).astype(jnp.bfloat16)
        for k, ln in enumerate(lanes):
            acc_q[b * block : high, ln] = rest[k * block : (k + 1) * block]
            wq[stage_rows(part_at, b * block, block), ln] = first[k * block : (k + 1) * block]

    def attend_rest(g, ln):
        count = (blocks - 2) * block
        more = jnp.dot(
            wq[stage_rows(part_at, block, count), ln],
            values_ref[g, :block, :HEAD_SIZE],
            preferred_element_type=jnp.float32,
        )
        whole = acc_q[block : block + count, ln] + more
        wq[stage_rows(stage_at, block, count), ln] = whole.astype(jnp.bfloat16)

    cut = total - block

    def out_copy(q, which):
        first, count = (0, cut) if which == 0 else (cut, block)
        lanes = pl.ds(pl.multiple_of(q * batch * HEAD_SIZE, batch * HEAD_SIZE), batch * HEAD_SIZE)
        return pltpu.make_async_copy(
            wq.at[stage_rows(stage_at, first, count), lanes],
            out_ref.at[pl.ds(first, count), lanes],
            out_sem.at[which, q],
        )

    def heads(body, which, q):
        g = q * batch // per_kv
        for pair in range(batch // 2):
            body(g, [lanes_of(q * batch + 2 * pair + k) for k in range(2)])
        out_copy(q, which).start()

    def over_heads(body, which):
        @pl.loop(0, head_local // batch)
        def _(q):
            heads(body, which, q)

    def early_keyval():
        keyval_copy(early_start, early_count, 0).wait_recv()
        gather_keys(early_start, early_count)
        gather_values(early_start, early_count)

        @pl.when(ends_first)
        def _():
            @pl.when(holds_values)
            def _():
                keyval_copy(late_start, rows, 1).wait_recv()

            gather_keys(late_start, rows)

    def early_attention(q):
        @pl.when(starts_first)
        def _():
            def body(g, lanes):
                for b in range(blocks - 1):
                    attend(b, g, lanes)

            heads(body, 0, q)

        @pl.when(ends_first)
        def _():
            def body(g, lanes):
                attend(blocks - 1, g, lanes)
                for b in range(1, blocks - 1):
                    attend_part(b, g, lanes)

            heads(body, 1, q)

    def late_attention():
        @pl.when(starts_first)
        def _():
            keyval_copy(late_start, rows, 1).wait_recv()
            gather_keys(late_start, rows)
            gather_values(late_start, rows)

            def body(g, lanes):
                attend(blocks - 1, g, lanes)

            over_heads(body, 1)

        @pl.when(ends_first)
        def _():
            @pl.when(holds_keys)
            def _():
                keyval_copy(late_start, rows, 1).wait_recv()

            gather_values(late_start, rows)

            def body(g, lanes):
                attend(0, g, lanes)
                for ln in lanes:
                    attend_rest(g, ln)

            over_heads(body, 0)

    for g in range(kv_used):
        values_ref[g, :, HEAD_SIZE:] = jnp.ones((total, HEAD_SIZE), jnp.bfloat16)

    @pl.loop(0, (n - 1) * chunks)
    def _(step):
        here = tuple(step < reach[side] * chunks for side in range(2))
        places = [item(reach[side], step) for side in range(2)]
        for side in range(2):
            p, i = places[side]

            @pl.when(here[side])
            def _():
                arrival(side, p, i).wait_recv()

            sends = (reach[side] + 1) * chunks
            head = (reach[side] + 1) * share

            @pl.when(jnp.logical_and(can_send[side], step + depth < sends))
            def _():
                send_item(side, step, False).wait_send()

                @pl.when(step + ahead <= head)
                def _():
                    start_send(side, step + ahead)

                @pl.when(step + ahead == head)
                def _():
                    for j in range(1, depth - 1):
                        start_send(side, step + ahead + j)

                @pl.when(step + ahead > head)
                def _():
                    start_send(side, step + depth)

        @pl.when(step < chunks // 2)
        def _():
            for c in (step, chunks - 1 - step):
                for copy in weight_copies(c):
                    copy.wait()

            @pl.when(step + 1 < chunks // 2)
            def _():
                start_weights(step + 1)

        for side in range(2):
            p, i = places[side]

            @pl.when(here[side])
            def _():
                keyval_unit(place(side, i), t - p if side == 0 else t + p)

        @pl.when(jnp.logical_and(is_end, step == last_step))
        def _():
            finish_late()

        for side in range(2):
            p, i = places[side]

            @pl.when(here[side])
            def _():
                query_unit(place(side, i), t - p if side == 0 else t + p)

        @pl.when(jnp.logical_and(step >= chunks, step < 2 * chunks))
        def _():
            keyval_unit(step - chunks, t)
            query_unit(step - chunks, t)

        @pl.when(step == chunks - 2)
        def _():
            fill_tables()

        @pl.when(step == low_at)
        def _():
            low_first()

        @pl.when(step == second_at)
        def _():
            low_second()

        @pl.when(step == third_at)
        def _():
            low_third()

        @pl.when(step == third_at)
        def _():
            finish_keyval(early_start, early_count)
            keyval_copy(early_start, early_count, 0).start()

            @pl.when(is_inner)
            def _():
                finish_late()

        @pl.when(step == early_at)
        def _():
            early_keyval()

        @pl.when(jnp.logical_and(step >= early_at, step < early_at + head_local // batch))
        def _():
            early_attention(step - early_at)

    late_attention()

    for copy in adapter_sends:
        copy.wait_send()
    for d in range(1, n):
        part_copy(d).wait_send()
        low_copy(d).wait_send()
    keyval_copy(early_start, early_count, 0).wait_send()
    keyval_copy(late_start, rows, 1).wait_send()

    for side in range(2):

        @pl.when(can_send[side])
        def _():
            for j in range(depth):
                send_item(side, (reach[side] + 1) * chunks - depth + j, False).wait_send()

    @pl.loop(0, head_local // batch)
    def _(q):
        for which in range(2):
            out_copy(q, which).wait()


def on_device(
    tokens,
    query_weight,
    key_value_weight,
    adapter_down_maps,
    adapter_up_query,
    adapter_up_key_value,
    adapter_row_table,
    request_adapter_ids,
    token_request_ids,
):
    n = lax.axis_size("tensor")
    stores = lax.axis_size("store")
    slots = adapter_down_maps.shape[0]
    rows, model_width = tokens.shape
    total = rows * n
    query_width = query_weight.shape[1]
    keyval_width = key_value_weight.shape[1]
    chunks = max(8, 2 * n)
    width = model_width // chunks
    pair_heads = keyval_width // HEAD_SIZE
    kv_used = max(query_width // HEAD_SIZE // (QUERY_HEADS // KEY_VALUE_HEADS), 1)
    two_ranks = 2 * ADAPTER_RANK
    hbm = pl.BlockSpec(memory_space=pl.ANY)
    vmem = pl.BlockSpec(memory_space=pltpu.VMEM)
    smem = pl.BlockSpec(memory_space=pltpu.SMEM)
    dma = pltpu.SemaphoreType.DMA
    return pl.pallas_call(
        functools.partial(project_kernel, n, stores, chunks, slots),
        in_specs=[hbm] * 6 + [smem, smem, vmem],
        out_specs=[hbm] * 4,
        out_shape=[
            jax.ShapeDtypeStruct((total, query_width), jnp.bfloat16),
            jax.ShapeDtypeStruct((stores, two_ranks, query_width), jnp.bfloat16),
            jax.ShapeDtypeStruct((stores, ADAPTER_RANK, query_width), jnp.bfloat16),
            jax.ShapeDtypeStruct((stores, ADAPTER_RANK, keyval_width), jnp.bfloat16),
        ],
        scratch_shapes=[
            pltpu.VMEM((chunks, total, width), jnp.bfloat16),
            pltpu.VMEM((model_width, query_width), jnp.bfloat16),
            pltpu.VMEM((model_width, keyval_width), jnp.bfloat16),
            pltpu.VMEM((total, query_width), jnp.float32),
            pltpu.VMEM((total, keyval_width), jnp.float32),
            pltpu.VMEM((stores, two_ranks, model_width // n), jnp.bfloat16),
            pltpu.VMEM((stores * ADAPTER_RANK, query_width), jnp.bfloat16),
            pltpu.VMEM((stores * ADAPTER_RANK, keyval_width), jnp.bfloat16),
            pltpu.VMEM((total, two_ranks), jnp.bfloat16),
            pltpu.VMEM((total, two_ranks), jnp.float32),
            pltpu.VMEM((n, rows, two_ranks), jnp.bfloat16),
            pltpu.VMEM((total, two_ranks), jnp.bfloat16),
            pltpu.VMEM((pair_heads, total, HEAD_SIZE), jnp.bfloat16),
            pltpu.VMEM((kv_used, total, HEAD_SIZE), jnp.bfloat16),
            pltpu.VMEM((kv_used, total, HEAD_SIZE), jnp.bfloat16),
            pltpu.VMEM((kv_used, total, 2 * HEAD_SIZE), jnp.bfloat16),
            pltpu.VMEM((total, total), jnp.float32),
            pltpu.VMEM((total, HEAD_SIZE), jnp.float32),
            pltpu.VMEM((total, HEAD_SIZE), jnp.float32),
            pltpu.VMEM((total, 1), jnp.float32),
            dma((chunks,)),
            dma((2, chunks)),
            dma((2, n, chunks)),
            dma((2, n, chunks)),
            dma((3, stores)),
            dma((3, stores)),
            dma((3,)),
            dma((3, slots)),
            dma((3, stores)),
            dma((n,)),
            dma((n,)),
            dma((n,)),
            dma((n,)),
            dma((2, 2)),
            dma((2, query_width // HEAD_SIZE)),
        ],
        compiler_params=pltpu.CompilerParams(
            collective_id=0, has_side_effects=True, vmem_limit_bytes=67043328
        ),
        name="project",
    )(
        tokens,
        query_weight,
        key_value_weight,
        adapter_down_maps,
        adapter_up_query,
        adapter_up_key_value,
        adapter_row_table,
        request_adapter_ids,
        token_request_ids,
    )[0]


def solution(mesh):
    return jax.shard_map(
        on_device,
        mesh=mesh,
        in_specs=(
            P(("groups", "store", "tensor"), None),
            P(None, "tensor"),
            P(None, "tensor"),
            P("store", None, "tensor"),
            P("store", None, "tensor"),
            P("store", None, "tensor"),
            P("groups"),
            P("groups", None),
            P(("groups", "store"), None),
        ),
        out_specs=P(("groups", "store"), "tensor"),
        check_vma=False,
    )
```

time: 172 us -> 166 us (0.965); the launches traced: 172 us -> 163 us
  Pallas kernels: 169 us -> 160 us
    pallas_call x2 -> x1, Pallas kernels: 169 us -> 160 us  [on_device(): pl.pallas_call(functools.partial(project_kernel, n, stores, chunks, slots...]
where the time goes in v1:
time: 166 us; the launch traced here: 163 us
  Pallas kernels  160 us (96%)
  local copies, waits for them, and re-layouts  3.16 us (2%)
    pallas_call x1, Pallas kernels, on_device(): pl.pallas_call(functools.partial(project_kernel, n, stores, chunks, slots...  160 us

profile of v1, /device:TPU:0, one launch (start us, length us, event | category | flops | bytes accessed | tf_op | source)
XLA Modules:
  0.0 163.3 jit_solution(4364852489644496142)
XLA Ops:
  0.0 160.2 %project.1 = (bf16[512,2048]{1,0:T(8,128)(2,1)}, bf16[4,128,2048]{2,1,0:T(8,128)(2,1)}, bf16[4,64,2048]{2,1,0:T(8,128)(2,1)}, bf16[4,64,512]{2,1,0:T(8,128)(2,1)}) custom-call(bf16[128,8192]{1,0:T(8,128)(2,1)} %tokens_ref.1, bf16[8192,2048]{1,0:T(8,128)(2,1)} %wq_hbm.1, bf16[8192,512]{1,0:T(8,128)(2,1)} %wkv_hbm.1, bf16[8,128,2048]{2,1,0:T(8,128)(2,1)} %down_hbm.1, ...), custom_call_target="tpu_custom_call" | custom-call | tf_op jit(solution)/shard_map/project/pallas_call | solution.py:841
  160.2 3.2 %copy.11 = bf16[512,2048]{1,0:T(8,128)(2,1)} copy(bf16[512,2048]{1,0:T(8,128)(2,1)} %get-tuple-element.6) | data formatting | bytes 4194304

commit v2 on v1

--- a/solution.py
+++ b/solution.py
@@ -362,19 +362,26 @@
 
     last_step = (n - 1) * chunks - 1
     inner_done = (n - 2) * chunks - 1
-    second_at = inner_done + jnp.where(is_end, 1, 0)
-    third_at = jnp.where(is_end, last_step - 3, inner_done + 1)
-    early_at = jnp.where(is_end, last_step - 2, last_step - 3)
+    third_at = jnp.where(is_end, last_step - 4, inner_done + 1)
+    early_at = last_step - jnp.where(is_end, 4, 3)
     low_at = jnp.maximum(jnp.maximum(low_ready(0), low_ready(1)), chunks)
 
-    def part_copy(d):
-        to = lax.rem(t + d, n)
+    pairs = n // 2
+    owners = [2 * m + 1 if 2 * m + 1 < n - 2 * m - 1 else 2 * m for m in range(pairs)]
+    own_pair = t // 2
+    is_owner = t == 2 * own_pair + jnp.where(2 * own_pair + 1 < n - 2 * own_pair - 1, 1, 0)
+
+    def pair_rows(m):
+        start = m * 2 * rows
+        return pl.ds(start if isinstance(m, int) else pl.multiple_of(start, 2 * rows), 2 * rows)
+
+    def part_copy(m):
         return pltpu.make_async_remote_copy(
-            src_ref=low_part.at[pl.ds(to * rows, rows), :],
+            src_ref=low_part.at[pair_rows(m), :],
             dst_ref=low_got.at[t],
-            send_sem=part_send.at[d],
-            recv_sem=part_recv.at[d],
-            device_id={"tensor": to},
+            send_sem=part_send.at[m],
+            recv_sem=part_recv.at[t],
+            device_id={"tensor": owners[m]},
             device_id_type=MESH,
         )
 
@@ -383,33 +390,31 @@
         return pltpu.make_async_remote_copy(
             src_ref=low_got.at[source],
             dst_ref=low_got.at[source],
-            send_sem=part_send.at[d],
-            recv_sem=part_recv.at[d],
+            send_sem=part_send.at[0],
+            recv_sem=part_recv.at[source],
             device_id={"tensor": source},
             device_id_type=MESH,
         )
 
     def low_copy(d):
-        to = lax.rem(t + d, n)
-        held = low_all.at[pl.ds(t * rows, rows), :]
+        held = low_all.at[pair_rows(own_pair), :]
         return pltpu.make_async_remote_copy(
             src_ref=held,
             dst_ref=held,
             send_sem=low_send.at[d],
-            recv_sem=low_recv.at[d],
-            device_id={"tensor": to},
+            recv_sem=low_recv.at[own_pair],
+            device_id={"tensor": lax.rem(t + d, n)},
             device_id_type=MESH,
         )
 
-    def low_arrival(d):
-        source = lax.rem(t + n - d, n)
-        held = low_all.at[pl.ds(source * rows, rows), :]
+    def low_arrival(m):
+        held = low_all.at[pair_rows(m), :]
         return pltpu.make_async_remote_copy(
             src_ref=held,
             dst_ref=held,
-            send_sem=low_send.at[d],
-            recv_sem=low_recv.at[d],
-            device_id={"tensor": source},
+            send_sem=low_send.at[0],
+            recv_sem=low_recv.at[m],
+            device_id={"tensor": owners[m]},
             device_id_type=MESH,
         )
 
@@ -443,11 +448,14 @@
             summed += picked * mask_of(p)
         low_part[...] = summed.astype(jnp.bfloat16)
         low_own[...] = summed
-        for d in range(1, n):
-            part_copy(d).start()
+        for m in range(pairs):
+
+            @pl.when(t != owners[m])
+            def _():
+                part_copy(m).start()
 
     def low_second():
-        at = pl.ds(pl.multiple_of(t * rows, rows), rows)
+        at = pair_rows(own_pair)
         whole = low_own[at, :]
         for d in range(1, n):
             part_arrival(d).wait_recv()
@@ -456,27 +464,33 @@
         for d in range(1, n):
             low_copy(d).start()
 
-    def low_third():
-        for d in range(1, n):
-            low_arrival(d).wait_recv()
+    def spread_low(lower):
         low = low_all[...].astype(jnp.float32)
         turned = pltpu.roll(low, ADAPTER_RANK, 1)
         in_lower = lax.broadcasted_iota(jnp.int32, low.shape, 1) < ADAPTER_RANK
-        twice_q = jnp.where(in_lower, low, turned)
-        twice_kv = jnp.where(in_lower, turned, low)
+        twice = jnp.where(in_lower, low, turned) if lower else jnp.where(in_lower, turned, low)
         masks = [
-            jnp.where(in_lower, mask_of(2 * p), mask_of(2 * p + 1))
-            for p in range(stores // 2)
+            jnp.where(in_lower, mask_of(2 * p), mask_of(2 * p + 1)) for p in range(stores // 2)
         ]
-        spread_q = jnp.concatenate([(twice_q * m).astype(jnp.bfloat16) for m in masks], axis=1)
-        spread_kv = jnp.concatenate([(twice_kv * m).astype(jnp.bfloat16) for m in masks], axis=1)
+        return jnp.concatenate([(twice * m).astype(jnp.bfloat16) for m in masks], axis=1)
+
+    def low_keyval():
+        for m in range(pairs):
+
+            @pl.when(t != owners[m])
+            def _():
+                low_arrival(m).wait_recv()
+
         acc_kv[...] += adapter_scale * jnp.dot(
-            spread_kv, upkv[...], preferred_element_type=jnp.float32
-        )
+            spread_low(False), upkv[...], preferred_element_type=jnp.float32
+        )
+
+    def low_query():
+        spread = spread_low(True)
         for k in range(query_width // tile_q):
             columns = slice(k * tile_q, (k + 1) * tile_q)
             acc_q[:, columns] += adapter_scale * jnp.dot(
-                spread_q, upq[:, columns], preferred_element_type=jnp.float32
+                spread, upq[:, columns], preferred_element_type=jnp.float32
             )
 
     def rotated(value, cosine, sine):
@@ -705,7 +719,7 @@
             sends = (reach[side] + 1) * chunks
             head = (reach[side] + 1) * share
 
-            @pl.when(jnp.logical_and(can_send[side], step + depth < sends))
+            @pl.when(jnp.logical_and(can_send[side], step + depth - 1 < sends))
             def _():
                 send_item(side, step, False).wait_send()
 
@@ -718,9 +732,13 @@
                     for j in range(1, depth - 1):
                         start_send(side, step + ahead + j)
 
-                @pl.when(step + ahead > head)
+                nearer = step > inner_done
+                later = step + depth - jnp.where(nearer, 1, 0)
+                wanted = jnp.logical_and(step + ahead > head, step != inner_done + 1)
+
+                @pl.when(jnp.logical_and(wanted, later < sends))
                 def _():
-                    start_send(side, step + depth)
+                    start_send(side, later)
 
         @pl.when(step < chunks // 2)
         def _():
@@ -763,16 +781,13 @@
         def _():
             low_first()
 
-        @pl.when(step == second_at)
+        @pl.when(jnp.logical_and(is_owner, step == inner_done))
         def _():
             low_second()
 
         @pl.when(step == third_at)
         def _():
-            low_third()
-
-        @pl.when(step == third_at)
-        def _():
+            low_keyval()
             finish_keyval(early_start, early_count)
             keyval_copy(early_start, early_count, 0).start()
 
@@ -780,6 +795,8 @@
             def _():
                 finish_late()
 
+            low_query()
+
         @pl.when(step == early_at)
         def _():
             early_keyval()
@@ -792,9 +809,17 @@
 
     for copy in adapter_sends:
         copy.wait_send()
-    for d in range(1, n):
-        part_copy(d).wait_send()
-        low_copy(d).wait_send()
+    for m in range(pairs):
+
+        @pl.when(t != owners[m])
+        def _():
+            part_copy(m).wait_send()
+
+    @pl.when(is_owner)
+    def _():
+        for d in range(1, n):
+            low_copy(d).wait_send()
+
     keyval_copy(early_start, early_count, 0).wait_send()
     keyval_copy(late_start, rows, 1).wait_send()
 
@@ -802,7 +827,7 @@
 
         @pl.when(can_send[side])
         def _():
-            for j in range(depth):
+            for j in range(1, depth):
                 send_item(side, (reach[side] + 1) * chunks - depth + j, False).wait_send()
 
     @pl.loop(0, head_local // batch)
@@ -838,7 +863,7 @@
     vmem = pl.BlockSpec(memory_space=pltpu.VMEM)
     smem = pl.BlockSpec(memory_space=pltpu.SMEM)
     dma = pltpu.SemaphoreType.DMA
-    return pl.pallas_call(
+    results = pl.pallas_call(
         functools.partial(project_kernel, n, stores, chunks, slots),
         in_specs=[hbm] * 6 + [smem, smem, vmem],
         out_specs=[hbm] * 4,
@@ -859,7 +884,7 @@
             pltpu.VMEM((stores * ADAPTER_RANK, keyval_width), jnp.bfloat16),
             pltpu.VMEM((total, two_ranks), jnp.bfloat16),
             pltpu.VMEM((total, two_ranks), jnp.float32),
-            pltpu.VMEM((n, rows, two_ranks), jnp.bfloat16),
+            pltpu.VMEM((n, 2 * rows, two_ranks), jnp.bfloat16),
             pltpu.VMEM((total, two_ranks), jnp.bfloat16),
             pltpu.VMEM((pair_heads, total, HEAD_SIZE), jnp.bfloat16),
             pltpu.VMEM((kv_used, total, HEAD_SIZE), jnp.bfloat16),
@@ -899,7 +924,45 @@
         adapter_row_table,
         request_adapter_ids,
         token_request_ids,
-    )[0]
+    )
+    return hand_over(results[0])
+
+
+def hand_over_kernel(pieces, source, out, held, in_sem, out_sem):
+    count = held.shape[0] // pieces
+
+    def load(k):
+        at = pl.ds(k * count, count)
+        return pltpu.make_async_copy(source.at[at, :], held.at[at, :], in_sem.at[k])
+
+    def store(k):
+        at = pl.ds(k * count, count)
+        return pltpu.make_async_copy(held.at[at, :], out.at[at, :], out_sem.at[k])
+
+    for k in range(pieces):
+        load(k).start()
+    for k in range(pieces):
+        load(k).wait()
+        store(k).start()
+    for k in range(pieces):
+        store(k).wait()
+
+
+def hand_over(attention):
+    hbm = pl.BlockSpec(memory_space=pl.ANY)
+    pieces = 8
+    return pl.pallas_call(
+        functools.partial(hand_over_kernel, pieces),
+        in_specs=[hbm],
+        out_specs=hbm,
+        out_shape=jax.ShapeDtypeStruct(attention.shape, attention.dtype),
+        scratch_shapes=[
+            pltpu.VMEM(attention.shape, attention.dtype),
+            pltpu.SemaphoreType.DMA((pieces,)),
+            pltpu.SemaphoreType.DMA((pieces,)),
+        ],
+        name="hand_over",
+    )(attention)
 
 
 def solution(mesh):

time: 166 us -> 161 us (0.970); the launches traced: 163 us -> 160 us
  local copies, waits for them, and re-layouts: 3.16 us -> 0 us
    unnamed x1 -> x0, local copies, waits for them, and re-layouts: 3.16 us -> none
    pallas_call x1, Pallas kernels: 160 us -> 158 us  [on_device(): pl.pallas_call(functools.partial(project_kernel, n, stores, chunks, slots...]
    pallas_call x0 -> x1, Pallas kernels: none -> 2.39 us  [hand_over(): pl.pallas_call(functools.partial(hand_over_kernel, pieces), in_specs=[hbm...]
where the time goes in v2:
time: 161 us; the launch traced here: 160 us
  Pallas kernels  160 us (99%)
    pallas_call x1, Pallas kernels, on_device(): pl.pallas_call(functools.partial(project_kernel, n, stores, chunks, slots...  158 us

profile of v2, /device:TPU:0, one launch (start us, length us, event | category | flops | bytes accessed | tf_op | source)
XLA Modules:
  0.0 160.2 jit_solution(5636398182047709088)
XLA Ops:
  0.0 157.7 %project.1 = (bf16[512,2048]{1,0:T(8,128)(2,1)}, bf16[4,128,2048]{2,1,0:T(8,128)(2,1)}, bf16[4,64,2048]{2,1,0:T(8,128)(2,1)}, bf16[4,64,512]{2,1,0:T(8,128)(2,1)}) custom-call(bf16[128,8192]{1,0:T(8,128)(2,1)} %tokens_ref.1, bf16[8192,2048]{1,0:T(8,128)(2,1)} %wq_hbm.1, bf16[8192,512]{1,0:T(8,128)(2,1)} %wkv_hbm.1, bf16[8,128,2048]{2,1,0:T(8,128)(2,1)} %down_hbm.1, ...), custom_call_target="tpu_custom_call" | custom-call | tf_op jit(solution)/shard_map/project/pallas_call | solution.py:866
  157.7 2.4 %hand_over.1 = bf16[512,2048]{1,0:T(8,128)(2,1)} custom-call(bf16[512,2048]{1,0:T(8,128)(2,1)} %get-tuple-element.6.source), custom_call_target="tpu_custom_call" | custom-call | tf_op jit(solution)/shard_map/hand_over/pallas_call | solution.py:954

commit v3 on v2

--- a/solution.py
+++ b/solution.py
@@ -77,6 +77,7 @@
     low_send,
     low_recv,
     kv_sem,
+    half_sem,
     out_sem,
 ):
     t = lax.axis_index("tensor")
@@ -95,10 +96,27 @@
         return rank * head_local // group_size - rank // 2 * pair_heads
 
     barrier = pltpu.get_barrier_semaphore()
+    pairs = n // 2
+    owners = [2 * m + 1 if 2 * m + 1 < n - 2 * m - 1 else 2 * m for m in range(pairs)]
+
+    def owns(rank):
+        m = rank // 2
+        return rank == 2 * m + jnp.where(2 * m + 1 < n - 2 * m - 1, 1, 0)
+
+    is_owner = owns(t)
+    greeted = 0
     for d in range(1, n):
-        pl.semaphore_signal(
-            barrier, inc=1, device_id={"tensor": lax.rem(t + d, n)}, device_id_type=MESH
-        )
+        peer = lax.rem(t + d, n)
+        near = jnp.logical_or(peer == t + 1, peer == t - 1)
+        meets = jnp.logical_or(near, jnp.logical_or(is_owner, owns(peer)))
+        greeted += jnp.where(meets, 1, 0)
+
+        @pl.when(meets)
+        def _():
+            pl.semaphore_signal(
+                barrier, inc=1, device_id={"tensor": peer}, device_id_type=MESH
+            )
+
     for d in range(1, stores):
         pl.semaphore_signal(
             barrier, inc=1, device_id={"store": lax.rem(s + d, stores)}, device_id_type=MESH
@@ -147,7 +165,7 @@
         for i, (source, held) in enumerate(adapter_pairs)
     ]
 
-    pl.semaphore_wait(barrier, n - 1 + stores - 1)
+    pl.semaphore_wait(barrier, greeted + stores - 1)
 
     def place(side, i):
         return chunks - 1 - i if side == 0 else i
@@ -198,14 +216,40 @@
         p, i = item(reach[side] + 1, j)
         return stream_copy(side, p - 1, i, own)
 
+    half = width // 2
+    last_chunk = jnp.where(t >= n - t, 0, chunks - 1)
+    last_shard = jnp.where(t >= n - t, 0, n - 1)
+    outward = jnp.where(t >= n - t, t + 1, t - 1)
+
+    def half_copy(h):
+        held = xbuf.at[
+            last_chunk,
+            pl.ds(pl.multiple_of(last_shard * rows, rows), rows),
+            pl.ds(h * half, half),
+        ]
+        return pltpu.make_async_remote_copy(
+            src_ref=held,
+            dst_ref=held,
+            send_sem=half_sem.at[0, h],
+            recv_sem=half_sem.at[1, h],
+            device_id={"tensor": jnp.where(is_end, t + 1 - 2 * (t % 2), outward)},
+            device_id_type=MESH,
+        )
+
     def start_send(side, j):
         p, i = item(reach[side] + 1, j)
+        is_last = jnp.logical_and(p == n - 1, i == chunks - 1)
+
+        @pl.when(is_last)
+        def _():
+            for h in range(2):
+                half_copy(h).start()
 
         @pl.when(p == 1)
         def _():
             stream_copy(side, 0, i, True).start()
 
-        @pl.when(p > 1)
+        @pl.when(jnp.logical_and(p > 1, jnp.logical_not(is_last)))
         def _():
             stream_copy(side, p - 1, i, False).start()
 
@@ -366,10 +410,7 @@
     early_at = last_step - jnp.where(is_end, 4, 3)
     low_at = jnp.maximum(jnp.maximum(low_ready(0), low_ready(1)), chunks)
 
-    pairs = n // 2
-    owners = [2 * m + 1 if 2 * m + 1 < n - 2 * m - 1 else 2 * m for m in range(pairs)]
     own_pair = t // 2
-    is_owner = t == 2 * own_pair + jnp.where(2 * own_pair + 1 < n - 2 * own_pair - 1, 1, 0)
 
     def pair_rows(m):
         start = m * 2 * rows
@@ -567,10 +608,8 @@
     def stage_rows(start, first, count):
         return pl.ds(pl.multiple_of(start + first, block), count)
 
-    def weights_of(b, g, lanes):
-        low = max(0, b * block - MAX_RUN)
-        high = (b + 1) * block
-        at = slice(b * block, high)
+    def scores_of(b, g, lanes, low, high):
+        at = slice(b * block, (b + 1) * block)
         query = [
             rotated(acc_q[at, ln], cos_ref[at, :], sin_ref[at, :]).astype(jnp.bfloat16)
             for ln in lanes
@@ -582,8 +621,12 @@
             preferred_element_type=jnp.float32,
         )
         scores = scores.reshape(2, block, high - low) + bias_ref[at, low:high][None]
-        scores = (scores - jnp.max(scores, axis=2, keepdims=True)) * scale
-        return jnp.exp2(scores).astype(jnp.bfloat16).reshape(2 * block, high - low)
+        return scores.reshape(2 * block, high - low)
+
+    def weights_of(b, g, lanes):
+        scores = scores_of(b, g, lanes, max(0, b * block - MAX_RUN), (b + 1) * block)
+        scores = (scores - jnp.max(scores, axis=1, keepdims=True)) * scale
+        return jnp.exp2(scores).astype(jnp.bfloat16)
 
     def attend(b, g, lanes):
         low = max(0, b * block - MAX_RUN)
@@ -599,28 +642,62 @@
         high = (b + 1) * block
         weights = weights_of(b, g, lanes)
         first = weights[:, :block]
-        mixed = jnp.dot(
-            weights[:, block:], values_ref[g, block:high, :], preferred_element_type=jnp.float32
-        )
-        sums = mixed[:, HEAD_SIZE:] + jnp.dot(
+        sums = jnp.dot(
             first, values_ref[g, :block, HEAD_SIZE:], preferred_element_type=jnp.float32
         )
+        if b > 0:
+            mixed = jnp.dot(
+                weights[:, block:], values_ref[g, block:high, :], preferred_element_type=jnp.float32
+            )
+            sums += mixed[:, HEAD_SIZE:]
         inverse = 1.0 / sums
-        rest = mixed[:, :HEAD_SIZE] * inverse
+        rest = mixed[:, :HEAD_SIZE] * inverse if b > 0 else jnp.zeros_like(inverse)
         first = (first.astype(jnp.float32) * inverse).astype(jnp.bfloat16)
         for k, ln in enumerate(lanes):
             acc_q[b * block : high, ln] = rest[k * block : (k + 1) * block]
             wq[stage_rows(part_at, b * block, block), ln] = first[k * block : (k + 1) * block]
 
-    def attend_rest(g, ln):
-        count = (blocks - 2) * block
+    def attend_rest(b, g, ln):
+        first, count = b * block, (blocks - 1 - b) * block
         more = jnp.dot(
-            wq[stage_rows(part_at, block, count), ln],
+            wq[stage_rows(part_at, first, count), ln],
             values_ref[g, :block, :HEAD_SIZE],
             preferred_element_type=jnp.float32,
         )
-        whole = acc_q[block : block + count, ln] + more
-        wq[stage_rows(stage_at, block, count), ln] = whole.astype(jnp.bfloat16)
+        whole = acc_q[first : first + count, ln] + more
+        wq[stage_rows(stage_at, first, count), ln] = whole.astype(jnp.bfloat16)
+
+    last = (blocks - 1) * block
+    kept = [slice(k * block, (k + 1) * block) for k in range(3)]
+
+    def attend_start(g, lanes):
+        scores = scores_of(blocks - 1, g, lanes, last - MAX_RUN, last)
+        top = jnp.max(scores, axis=1, keepdims=True)
+        weights = jnp.exp2((scores - top) * scale).astype(jnp.bfloat16)
+        mixed = jnp.dot(
+            weights, values_ref[g, last - MAX_RUN : last, :], preferred_element_type=jnp.float32
+        )
+        for k, ln in enumerate(lanes):
+            at = slice(k * block, (k + 1) * block)
+            acc_q[kept[0], ln] = mixed[at, :HEAD_SIZE]
+            acc_q[kept[1], ln] = mixed[at, HEAD_SIZE:]
+            acc_q[kept[2], ln] = jnp.broadcast_to(top[at], (block, HEAD_SIZE))
+
+    def attend_finish(g, lanes):
+        scores = scores_of(blocks - 1, g, lanes, last, total)
+        total_of, sum_of, top_of = (
+            jnp.concatenate([acc_q[at, ln] for ln in lanes], axis=0) for at in kept
+        )
+        top = jnp.maximum(top_of, jnp.max(scores, axis=1, keepdims=True))
+        weights = jnp.exp2((scores - top) * scale).astype(jnp.bfloat16)
+        shrink = jnp.exp2((top_of - top) * scale)
+        mixed = jnp.dot(
+            weights, values_ref[g, last:total, :], preferred_element_type=jnp.float32
+        )
+        sums = sum_of * shrink + mixed[:, HEAD_SIZE:]
+        mixed = ((total_of * shrink + mixed[:, :HEAD_SIZE]) / sums).astype(jnp.bfloat16)
+        for k, ln in enumerate(lanes):
+            wq[stage_rows(stage_at, last, block), ln] = mixed[k * block : (k + 1) * block]
 
     cut = total - block
 
@@ -658,35 +735,58 @@
             gather_keys(late_start, rows)
 
     def early_attention(q):
-        @pl.when(starts_first)
-        def _():
+        def lower(inner):
             def body(g, lanes):
                 for b in range(blocks - 1):
                     attend(b, g, lanes)
-
-            heads(body, 0, q)
-
-        @pl.when(ends_first)
-        def _():
+                if inner:
+                    attend_start(g, lanes)
+
+            return body
+
+        def upper(inner):
             def body(g, lanes):
                 attend(blocks - 1, g, lanes)
-                for b in range(1, blocks - 1):
+                for b in range(0 if inner else 1, blocks - 1):
                     attend_part(b, g, lanes)
 
-            heads(body, 1, q)
+            return body
+
+        for inner, where in ((False, is_end), (True, is_inner)):
+
+            @pl.when(jnp.logical_and(where, starts_first))
+            def _():
+                heads(lower(inner), 0, q)
+
+            @pl.when(jnp.logical_and(where, ends_first))
+            def _():
+                heads(upper(inner), 1, q)
 
     def late_attention():
+        def lower(inner):
+            def body(g, lanes):
+                if inner:
+                    attend_finish(g, lanes)
+                else:
+                    attend(blocks - 1, g, lanes)
+
+            return body
+
+        def upper(inner):
+            def body(g, lanes):
+                if not inner:
+                    attend(0, g, lanes)
+                for ln in lanes:
+                    attend_rest(0 if inner else 1, g, ln)
+
+            return body
+
         @pl.when(starts_first)
         def _():
             keyval_copy(late_start, rows, 1).wait_recv()
             gather_keys(late_start, rows)
             gather_values(late_start, rows)
 
-            def body(g, lanes):
-                attend(blocks - 1, g, lanes)
-
-            over_heads(body, 1)
-
         @pl.when(ends_first)
         def _():
             @pl.when(holds_keys)
@@ -695,17 +795,20 @@
 
             gather_values(late_start, rows)
 
-            def body(g, lanes):
-                attend(0, g, lanes)
-                for ln in lanes:
-                    attend_rest(g, ln)
-
-            over_heads(body, 0)
+        for inner, where in ((False, is_end), (True, is_inner)):
+
+            @pl.when(jnp.logical_and(where, starts_first))
+            def _():
+                over_heads(lower(inner), 1)
+
+            @pl.when(jnp.logical_and(where, ends_first))
+            def _():
+                over_heads(upper(inner), 0)
 
     for g in range(kv_used):
         values_ref[g, :, HEAD_SIZE:] = jnp.ones((total, HEAD_SIZE), jnp.bfloat16)
 
-    @pl.loop(0, (n - 1) * chunks)
+    @pl.loop(0, last_step)
     def _(step):
         here = tuple(step < reach[side] * chunks for side in range(2))
         places = [item(reach[side], step) for side in range(2)]
@@ -757,10 +860,6 @@
             def _():
                 keyval_unit(place(side, i), t - p if side == 0 else t + p)
 
-        @pl.when(jnp.logical_and(is_end, step == last_step))
-        def _():
-            finish_late()
-
         for side in range(2):
             p, i = places[side]
 
@@ -804,6 +903,26 @@
         @pl.when(jnp.logical_and(step >= early_at, step < early_at + head_local // batch))
         def _():
             early_attention(step - early_at)
+
+    @pl.when(is_end)
+    def _():
+        at = pl.ds(late_start, rows)
+        for h in range(2):
+            half_copy(h).wait_recv()
+            part = pl.ds(pl.multiple_of(last_chunk * width + h * half, half), half)
+            x = xbuf[last_chunk, at, h * half : (h + 1) * half]
+            acc_kv[at, :] += jnp.dot(x, wkv[part, :], preferred_element_type=jnp.float32)
+            if h == 1:
+                finish_late()
+
+            @pl.loop(0, query_width // tile_q)
+            def _(k):
+                columns = pl.ds(pl.multiple_of(k * tile_q, tile_q), tile_q)
+                acc_q[at, columns] += jnp.dot(
+                    xbuf[last_chunk, at, h * half : (h + 1) * half],
+                    wq[part, columns],
+                    preferred_element_type=jnp.float32,
+                )
 
     late_attention()
 
@@ -827,8 +946,17 @@
 
         @pl.when(can_send[side])
         def _():
-            for j in range(1, depth):
+            for j in range(1, depth - 1):
                 send_item(side, (reach[side] + 1) * chunks - depth + j, False).wait_send()
+
+            @pl.when(reach[side] < n - 2)
+            def _():
+                send_item(side, (reach[side] + 1) * chunks - 1, False).wait_send()
+
+            @pl.when(reach[side] == n - 2)
+            def _():
+                for h in range(2):
+                    half_copy(h).wait_send()
 
     @pl.loop(0, head_local // batch)
     def _(q):
@@ -908,6 +1036,7 @@
             dma((n,)),
             dma((n,)),
             dma((2, 2)),
+            dma((2, 2)),
             dma((2, query_width // HEAD_SIZE)),
         ],
         compiler_params=pltpu.CompilerParams(

time: 161 us -> 160 us (level)
  no operation moved by 1% of the time
where the time goes in v3:
time: 160 us
  Pallas kernels  159 us (99%)
    pallas_call x1, Pallas kernels, on_device(): pl.pallas_call(functools.partial(project_kernel, n, stores, chunks, slots...  157 us

profile of v3, /device:TPU:0, one launch (start us, length us, event | category | flops | bytes accessed | tf_op | source)
XLA Modules:
  0.0 159.6 jit_solution(13134647479972028970)
XLA Ops:
  0.0 157.1 %project.1 = (bf16[512,2048]{1,0:T(8,128)(2,1)}, bf16[4,128,2048]{2,1,0:T(8,128)(2,1)}, bf16[4,64,2048]{2,1,0:T(8,128)(2,1)}, bf16[4,64,512]{2,1,0:T(8,128)(2,1)}) custom-call(bf16[128,8192]{1,0:T(8,128)(2,1)} %tokens_ref.1, bf16[8192,2048]{1,0:T(8,128)(2,1)} %wq_hbm.1, bf16[8192,512]{1,0:T(8,128)(2,1)} %wkv_hbm.1, bf16[8,128,2048]{2,1,0:T(8,128)(2,1)} %down_hbm.1, ...), custom_call_target="tpu_custom_call" | custom-call | tf_op jit(solution)/shard_map/project/pallas_call | solution.py:994
  157.1 2.4 %hand_over.1 = bf16[512,2048]{1,0:T(8,128)(2,1)} custom-call(bf16[512,2048]{1,0:T(8,128)(2,1)} %get-tuple-element.6.source), custom_call_target="tpu_custom_call" | custom-call | tf_op jit(solution)/shard_map/hand_over/pallas_call | solution.py:1083

commit v4 on v3

--- a/solution.py
+++ b/solution.py
@@ -59,6 +59,7 @@
     kv_got,
     keys_ref,
     values_ref,
+    twin_ref,
     bias_ref,
     cos_ref,
     sin_ref,
@@ -657,11 +658,12 @@
             acc_q[b * block : high, ln] = rest[k * block : (k + 1) * block]
             wq[stage_rows(part_at, b * block, block), ln] = first[k * block : (k + 1) * block]
 
-    def attend_rest(b, g, ln):
+    def attend_rest(b, g, lanes):
+        ln = pl.ds(lanes[0].start, 2 * HEAD_SIZE)
         first, count = b * block, (blocks - 1 - b) * block
         more = jnp.dot(
             wq[stage_rows(part_at, first, count), ln],
-            values_ref[g, :block, :HEAD_SIZE],
+            twin_ref[g],
             preferred_element_type=jnp.float32,
         )
         whole = acc_q[first : first + count, ln] + more
@@ -776,8 +778,7 @@
             def body(g, lanes):
                 if not inner:
                     attend(0, g, lanes)
-                for ln in lanes:
-                    attend_rest(0 if inner else 1, g, ln)
+                attend_rest(0 if inner else 1, g, lanes)
 
             return body
 
@@ -794,6 +795,10 @@
                 keyval_copy(late_start, rows, 1).wait_recv()
 
             gather_values(late_start, rows)
+            for g in range(kv_used):
+                value = values_ref[g, :block, :HEAD_SIZE]
+                twin_ref[g, :block, :HEAD_SIZE] = value
+                twin_ref[g, block:, HEAD_SIZE:] = value
 
         for inner, where in ((False, is_end), (True, is_inner)):
 
@@ -805,6 +810,7 @@
             def _():
                 over_heads(upper(inner), 0)
 
+    twin_ref[...] = jnp.zeros_like(twin_ref)
     for g in range(kv_used):
         values_ref[g, :, HEAD_SIZE:] = jnp.ones((total, HEAD_SIZE), jnp.bfloat16)
 
@@ -1018,6 +1024,7 @@
             pltpu.VMEM((kv_used, total, HEAD_SIZE), jnp.bfloat16),
             pltpu.VMEM((kv_used, total, HEAD_SIZE), jnp.bfloat16),
             pltpu.VMEM((kv_used, total, 2 * HEAD_SIZE), jnp.bfloat16),
+            pltpu.VMEM((kv_used, 2 * HEAD_SIZE, 2 * HEAD_SIZE), jnp.bfloat16),
             pltpu.VMEM((total, total), jnp.float32),
             pltpu.VMEM((total, HEAD_SIZE), jnp.float32),
             pltpu.VMEM((total, HEAD_SIZE), jnp.float32),

time: 160 us -> 160 us (level)
  no operation moved by 1% of the time
where the time goes in v4:
time: 160 us
  Pallas kernels  159 us (99%)
    pallas_call x1, Pallas kernels, on_device(): pl.pallas_call(functools.partial(project_kernel, n, stores, chunks, slots...  157 us

profile of v4, /device:TPU:0, one launch (start us, length us, event | category | flops | bytes accessed | tf_op | source)
XLA Modules:
  0.0 159.6 jit_solution(796099137436747518)
XLA Ops:
  0.0 157.1 %project.1 = (bf16[512,2048]{1,0:T(8,128)(2,1)}, bf16[4,128,2048]{2,1,0:T(8,128)(2,1)}, bf16[4,64,2048]{2,1,0:T(8,128)(2,1)}, bf16[4,64,512]{2,1,0:T(8,128)(2,1)}) custom-call(bf16[128,8192]{1,0:T(8,128)(2,1)} %tokens_ref.1, bf16[8192,2048]{1,0:T(8,128)(2,1)} %wq_hbm.1, bf16[8192,512]{1,0:T(8,128)(2,1)} %wkv_hbm.1, bf16[8,128,2048]{2,1,0:T(8,128)(2,1)} %down_hbm.1, ...), custom_call_target="tpu_custom_call" | custom-call | tf_op jit(solution)/shard_map/project/pallas_call | solution.py:1000
  157.1 2.4 %hand_over.1 = bf16[512,2048]{1,0:T(8,128)(2,1)} custom-call(bf16[512,2048]{1,0:T(8,128)(2,1)} %get-tuple-element.6.source), custom_call_target="tpu_custom_call" | custom-call | tf_op jit(solution)/shard_map/hand_over/pallas_call | solution.py:1090

commit v5 on v4

--- a/solution.py
+++ b/solution.py
@@ -60,6 +60,7 @@
     keys_ref,
     values_ref,
     twin_ref,
+    twin_keys_ref,
     bias_ref,
     cos_ref,
     sin_ref,
@@ -686,20 +687,32 @@
             acc_q[kept[2], ln] = jnp.broadcast_to(top[at], (block, HEAD_SIZE))
 
     def attend_finish(g, lanes):
-        scores = scores_of(blocks - 1, g, lanes, last, total)
-        total_of, sum_of, top_of = (
-            jnp.concatenate([acc_q[at, ln] for ln in lanes], axis=0) for at in kept
-        )
-        top = jnp.maximum(top_of, jnp.max(scores, axis=1, keepdims=True))
-        weights = jnp.exp2((scores - top) * scale).astype(jnp.bfloat16)
-        shrink = jnp.exp2((top_of - top) * scale)
+        at = slice(last, total)
+        query = [
+            rotated(acc_q[at, ln], cos_ref[at, :], sin_ref[at, :]).astype(jnp.bfloat16)
+            for ln in lanes
+        ]
+        both = lax.dot_general(
+            jnp.concatenate(query, axis=1),
+            twin_keys_ref[g],
+            (((1,), (1,)), ((), ())),
+            preferred_element_type=jnp.float32,
+        )
+        weights, shrinks, sums = [], [], []
+        for k, ln in enumerate(lanes):
+            scores = both[:, k * block : (k + 1) * block] + bias_ref[at, last:total]
+            top_of = acc_q[kept[2], ln]
+            top = jnp.maximum(top_of, jnp.max(scores, axis=1, keepdims=True))
+            weights.append(jnp.exp2((scores - top) * scale).astype(jnp.bfloat16))
+            shrinks.append(jnp.exp2((top_of - top) * scale))
+            more = jnp.sum(weights[k].astype(jnp.float32), axis=1, keepdims=True)
+            sums.append(acc_q[kept[1], ln] * shrinks[k] + more)
         mixed = jnp.dot(
-            weights, values_ref[g, last:total, :], preferred_element_type=jnp.float32
-        )
-        sums = sum_of * shrink + mixed[:, HEAD_SIZE:]
-        mixed = ((total_of * shrink + mixed[:, :HEAD_SIZE]) / sums).astype(jnp.bfloat16)
+            jnp.concatenate(weights, axis=1), twin_ref[g], preferred_element_type=jnp.float32
+        )
         for k, ln in enumerate(lanes):
-            wq[stage_rows(stage_at, last, block), ln] = mixed[k * block : (k + 1) * block]
+            whole = acc_q[kept[0], ln] * shrinks[k] + mixed[:, k * block : (k + 1) * block]
+            wq[stage_rows(stage_at, last, block), ln] = (whole / sums[k]).astype(jnp.bfloat16)
 
     cut = total - block
 
@@ -787,6 +800,11 @@
             keyval_copy(late_start, rows, 1).wait_recv()
             gather_keys(late_start, rows)
             gather_values(late_start, rows)
+            for g in range(kv_used):
+                for k in range(2):
+                    at = slice(k * block, (k + 1) * block)
+                    twin_ref[g, at, at] = values_ref[g, last:total, :HEAD_SIZE]
+                    twin_keys_ref[g, at, at] = keys_ref[g, last:total, :]
 
         @pl.when(ends_first)
         def _():
@@ -811,6 +829,7 @@
                 over_heads(upper(inner), 0)
 
     twin_ref[...] = jnp.zeros_like(twin_ref)
+    twin_keys_ref[...] = jnp.zeros_like(twin_keys_ref)
     for g in range(kv_used):
         values_ref[g, :, HEAD_SIZE:] = jnp.ones((total, HEAD_SIZE), jnp.bfloat16)
 
@@ -1025,6 +1044,7 @@
             pltpu.VMEM((kv_used, total, HEAD_SIZE), jnp.bfloat16),
             pltpu.VMEM((kv_used, total, 2 * HEAD_SIZE), jnp.bfloat16),
             pltpu.VMEM((kv_used, 2 * HEAD_SIZE, 2 * HEAD_SIZE), jnp.bfloat16),
+            pltpu.VMEM((kv_used, 2 * HEAD_SIZE, 2 * HEAD_SIZE), jnp.bfloat16),
             pltpu.VMEM((total, total), jnp.float32),
             pltpu.VMEM((total, HEAD_SIZE), jnp.float32),
             pltpu.VMEM((total, HEAD_SIZE), jnp.float32),

time: 160 us -> 160 us (level)
  no operation moved by 1% of the time
where the time goes in v5:
time: 160 us
  Pallas kernels  159 us (99%)
    pallas_call x1, Pallas kernels, on_device(): pl.pallas_call(functools.partial(project_kernel, n, stores, chunks, slots...  157 us

profile of v5, /device:TPU:0, one launch (start us, length us, event | category | flops | bytes accessed | tf_op | source)
XLA Modules:
  0.0 159.7 jit_solution(380895473295138203)
XLA Ops:
  0.0 157.1 %project.1 = (bf16[512,2048]{1,0:T(8,128)(2,1)}, bf16[4,128,2048]{2,1,0:T(8,128)(2,1)}, bf16[4,64,2048]{2,1,0:T(8,128)(2,1)}, bf16[4,64,512]{2,1,0:T(8,128)(2,1)}) custom-call(bf16[128,8192]{1,0:T(8,128)(2,1)} %tokens_ref.1, bf16[8192,2048]{1,0:T(8,128)(2,1)} %wq_hbm.1, bf16[8192,512]{1,0:T(8,128)(2,1)} %wkv_hbm.1, bf16[8,128,2048]{2,1,0:T(8,128)(2,1)} %down_hbm.1, ...), custom_call_target="tpu_custom_call" | custom-call | tf_op jit(solution)/shard_map/project/pallas_call | solution.py:1019
  157.1 2.4 %hand_over.1 = bf16[512,2048]{1,0:T(8,128)(2,1)} custom-call(bf16[512,2048]{1,0:T(8,128)(2,1)} %get-tuple-element.6.source), custom_call_target="tpu_custom_call" | custom-call | tf_op jit(solution)/shard_map/hand_over/pallas_call | solution.py:1110
